TPU v7x, 32 devices: a whole 2x2x4 slice. The times are simulated.
32 devices in a mesh: seq: 8 (over z, y), ch: 4 (over x, core).
Axes of the slice: x: 2, y: 2, z: 4, core: 2. Of those that a mesh axis runs over, the one named last changes fastest.
Arguments:
- mamba_in: bfloat16 [2048, 8192], P('seq', 'ch'), may hold values from -6 to 6
- gate_in: bfloat16 [2048, 8192], P('seq', 'ch'), may hold values from -6 to 6
- delta_in: bfloat16 [2048, 8192], P('seq', 'ch'), may hold values from -3 to 16
- step_bias: float32 [8192], P('ch'), may hold values from -12 to 1.5
- decay_log: float32 [8192, 16], P('ch'), may hold values from -3.9 to -1.6
- input_map_state: bfloat16 [2048, 16], P('seq'), may hold values from -6 to 6
- state_out: bfloat16 [2048, 16], P('seq'), may hold values from -1.5 to 1.5
- skip_gain: float32 [8192], P('ch'), may hold values from 0.5 to 1.5
- out_weight: bfloat16 [8192, 8192], P('ch'), may hold values from -0.0625 to 0.0625
- residual: bfloat16 [2048, 8192], P('seq', 'ch'), may hold values from -6 to 6
- norm_gain: bfloat16 [8192], P('ch'), may hold values from 0.5 to 1.5
- query_weight: bfloat16 [8192, 8192], P('seq', 'ch'), may hold values from -1 to 1
- key_weight: bfloat16 [8192, 1024], P('seq'), may hold values from -1 to 1
- value_weight: bfloat16 [8192, 1024], P('seq'), may hold values from -0.0625 to 0.0625
Outputs:
- mamba_out: bfloat16 [2048, 8192], P('seq', 'ch')
- attention_out: bfloat16 [2048, 8192], P('seq', 'ch')
All inputs are finite; a program needn't handle non-finite values.
Results may differ from a plain program's by a relative error of at most 0.01.
Values may be sent and summed in bfloat16 or wider, within the bound.
No kernel may reach another device: no remote copies, remote signals or barrier semaphores. Data moves between devices by JAX's collectives and lax.ppermute only.
A program may use at most 128 MiB of HBM per device.

v0:
```python
import math

import jax
import jax.numpy as jnp
from jax import lax
from jax.sharding import PartitionSpec as P

D = 8192
H = 64
KVH = 8
HD = 128


def entering_2(array, axis, combine, identity):
    devices, place = (lax.axis_size(axis), lax.axis_index(axis))
    everything = jax.tree.map(lambda part: lax.all_gather(part, axis), array)
    start = jax.tree.map(
        lambda part, zero: jnp.broadcast_to(jnp.asarray(zero, part.dtype), part.shape),
        array,
        identity,
    )

    def lap(k, before):
        reached = k < place
        new = combine(before, jax.tree.map(lambda part: part[k], everything))
        return jax.tree.map(lambda a, b: jnp.where(reached, a, b), new, before)

    return lax.fori_loop(0, devices, lap, start)


def project(normed, query_part, kv_part):
    starting = (
        jnp.zeros((normed.shape[0], query_part.shape[1]), jnp.float32),
        jnp.zeros((normed.shape[0], kv_part.shape[1]), jnp.float32),
    )
    pieces = (
        lax.all_gather(query_part, "seq", axis=0, tiled=True),
        lax.all_gather(kv_part, "seq", axis=0, tiled=True),
    )
    columns = lax.slice_in_dim(normed, 0, pieces[0].shape[0], axis=1)
    return (
        starting[0] + jnp.dot(columns, pieces[0], preferred_element_type=jnp.float32),
        starting[1] + jnp.dot(columns, pieces[1], preferred_element_type=jnp.float32),
    )


def both_heads(normed, query_weight, key_part, value_part):
    query_sums, kv_sums = project(
        normed, query_weight, jnp.concatenate([key_part, value_part], axis=1)
    )
    width = key_part.shape[1]
    kv_rows = kv_sums.astype(jnp.bfloat16)
    return (query_sums.astype(jnp.bfloat16), kv_rows[:, :width], kv_rows[:, width:])


def attend_heads(queries, key_rows, value_rows, kv_heads):
    tokens_here = queries.shape[0]
    grouped = queries.reshape(tokens_here, kv_heads, -1, HD)
    per_group = grouped.shape[2]
    query_pos = lax.axis_index("seq") * tokens_here + jnp.arange(tokens_here, dtype=jnp.int32)
    factor = 1.0 / math.sqrt(HD)
    starting = (
        jnp.full((kv_heads, per_group, tokens_here), -1e30, jnp.float32),
        jnp.zeros((kv_heads, per_group, tokens_here), jnp.float32),
        jnp.zeros((kv_heads, per_group, tokens_here, HD), jnp.float32),
    )
    pieces = (
        lax.all_gather(key_rows, "seq", axis=0, tiled=True),
        lax.all_gather(value_rows, "seq", axis=0, tiled=True),
    )
    count = pieces[0].shape[0]
    block_rows = math.gcd(count, 512)
    key_blocks = pieces[0].reshape(count // block_rows, block_rows, kv_heads, HD)
    value_blocks = pieces[1].reshape(count // block_rows, block_rows, kv_heads, HD)
    firsts = jnp.int32(0) + block_rows * jnp.arange(count // block_rows, dtype=jnp.int32)

    def one_block(state, inputs):
        key_block, value_block, first_key = inputs
        running_max, partial_total, weighted = state
        scores = (
            jnp.einsum("tkgd,skd->kgts", grouped, key_block, preferred_element_type=jnp.float32)
            * factor
        )
        allowed = (first_key + jnp.arange(block_rows, dtype=jnp.int32))[None, :] <= query_pos[
            :, None
        ]
        scores = jnp.where(allowed, scores, -1e30)
        new_max = jnp.maximum(running_max, jnp.max(scores, axis=3))
        rescale = jnp.exp(running_max - new_max)
        weights = jnp.where(allowed, jnp.exp(scores - new_max[..., None]), 0.0)
        partial_total = partial_total * rescale + jnp.sum(weights, axis=3)
        weighted = weighted * rescale[..., None] + jnp.einsum(
            "kgts,skd->kgtd",
            weights.astype(jnp.bfloat16),
            value_block,
            preferred_element_type=jnp.float32,
        )
        return ((new_max, partial_total, weighted), None)

    result, _ = lax.scan(one_block, starting, (key_blocks, value_blocks, firsts))
    _, partial_total, weighted = result
    heads = weighted / partial_total[..., None]
    return (
        jnp.transpose(heads, (2, 0, 1, 3))
        .reshape(tokens_here, kv_heads * per_group * HD)
        .astype(jnp.bfloat16)
    )


def shards(
    mamba_in,
    gate_in,
    delta_in,
    step_bias,
    decay_log,
    input_map_state,
    state_out,
    skip_gain,
    out_weight,
    residual,
    norm_gain,
    query_weight,
    key_weight,
    value_weight,
):
    tokens_here = mamba_in.shape[0]
    decay_rate = jnp.exp(decay_log)
    step_size = jax.nn.softplus(delta_in.astype(jnp.float32) + step_bias)
    drive_rows = mamba_in.astype(jnp.float32)
    input_rows = input_map_state.astype(jnp.float32)
    result_rows = state_out.astype(jnp.float32)
    outer = min(tokens_here, 16)
    inner = tokens_here // outer

    def advance_block(carried_state, inputs):
        block_steps, block_drive, block_in, block_out = inputs
        results = []
        for position in range(inner):
            carried_state = (
                jnp.exp(-block_steps[position][:, None] * decay_rate) * carried_state
                + (block_steps[position] * block_drive[position])[:, None]
                * block_in[position][None, :]
            )
            results.append(jnp.sum(carried_state * block_out[position][None, :], axis=1))
        return (carried_state, jnp.stack(results))

    reshaped_array = tuple(
        (
            array_in.reshape(outer, inner, array_in.shape[1])
            for array_in in (step_size, drive_rows, input_rows, result_rows)
        )
    )
    final_state, local_out = lax.scan(advance_block, jnp.zeros_like(decay_rate), reshaped_array)
    local_out = local_out.reshape(tokens_here, -1)
    span_total = jnp.sum(step_size, axis=0)

    def combine(earlier_part, later_part):
        return (
            earlier_part[0] + later_part[0],
            earlier_part[1] * jnp.exp(-later_part[0][:, None] * decay_rate) + later_part[1],
        )

    _, entering = entering_2(
        (span_total, final_state),
        "seq",
        combine,
        (jnp.zeros_like(span_total), jnp.zeros_like(final_state)),
    )
    cumulative = jnp.cumsum(step_size, axis=0)
    block_rows = math.gcd(tokens_here, 32)

    def carry_block(inputs):
        block_cum, block_out = inputs
        faded = jnp.exp(-block_cum[:, :, None] * decay_rate[None]) * entering[None]
        return jnp.sum(faded * block_out[:, None, :], axis=2)

    carried = lax.map(
        carry_block,
        (
            cumulative.reshape(-1, block_rows, cumulative.shape[1]),
            result_rows.reshape(-1, block_rows, result_rows.shape[1]),
        ),
    )
    scanned = local_out + carried.reshape(tokens_here, -1) + skip_gain * drive_rows
    gated = (scanned * jax.nn.silu(gate_in.astype(jnp.float32))).astype(jnp.bfloat16)
    partial_terms = jnp.dot(gated, out_weight, preferred_element_type=jnp.float32)
    projected = lax.psum_scatter(partial_terms, "ch", scatter_dimension=1, tiled=True)
    mamba_out = (residual.astype(jnp.float32) + projected).astype(jnp.bfloat16)
    local_rows = mamba_out.astype(jnp.float32)
    row_sums = lax.psum(jnp.sum(jnp.square(local_rows), axis=1), "ch")
    inverse_rms = lax.rsqrt(row_sums / D + 1e-06)
    normed_local = (local_rows * inverse_rms[:, None] * norm_gain.astype(jnp.float32)).astype(
        jnp.bfloat16
    )
    normed = lax.all_gather(normed_local, "ch", axis=1, tiled=True)
    query_heads = query_weight.shape[1] // HD
    group_size = H // KVH
    kv_heads = max(1, query_heads // group_size)
    first_head = lax.axis_index("ch") * query_heads // group_size
    key_part = lax.dynamic_slice_in_dim(key_weight, first_head * HD, kv_heads * HD, 1)
    value_part = lax.dynamic_slice_in_dim(value_weight, first_head * HD, kv_heads * HD, 1)
    queries, key_rows, value_rows = both_heads(normed, query_weight, key_part, value_part)
    attention_out = attend_heads(queries, key_rows, value_rows, kv_heads)
    return (mamba_out, attention_out)


def solution(mesh):
    return jax.shard_map(
        shards,
        mesh=mesh,
        in_specs=(
            P("seq", "ch"),
            P("seq", "ch"),
            P("seq", "ch"),
            P("ch"),
            P("ch", None),
            P("seq", None),
            P("seq", None),
            P("ch"),
            P("ch", None),
            P("seq", "ch"),
            P("ch"),
            P("seq", "ch"),
            P("seq", None),
            P("seq", None),
        ),
        out_specs=(P("seq", "ch"), P("seq", "ch")),
        check_vma=False,
    )
```

profile of v0, /device:TPU:0, one launch (start us, length us, event | category | flops | bytes accessed | tf_op | source)
XLA Modules:
  0.0 1254.4 jit_solution(13398187129990720063)
XLA Ops:
  8.3 2.8 convert.1
  12.0 2.0 fusion.96
  14.0 87.9 %while.53 = (s32[]{:T(128)}, f32[2048,16]{0,1:T(8,128)S(1)}, f32[16,16,2048]{2,1,0:T(8,128)}, f32[16,16,2048]{2,1,0:T(8,128)S(1)}, f32[2048,16]{0,1:T(8,128)S(1)...) while((s32[]{:T(128)}, f32[2048,16]{0,1:T(8,128)S(1)}, ...), condition=%wide.region_17.18_spmd.clone, body=%wide.region_0.17_spmd.clone.sunk | while | flops 4685842 | bytes 3989212 | solution.py:153
  14.0 1.9 fusion.116
  19.4 2.2 fusion.116
  25.0 1.9 fusion.116
  30.3 2.2 fusion.116
  36.0 1.9 fusion.116
  41.4 2.2 fusion.116
  47.1 1.9 fusion.116
  52.5 2.2 fusion.116
  58.2 1.9 fusion.116
  63.5 2.2 fusion.116
  69.2 1.9 fusion.116
  74.6 1.9 fusion.116
  80.0 1.9 fusion.116
  85.4 2.0 fusion.116
  90.8 2.0 fusion.116
  96.2 2.2 fusion.116
  102.7 32.8 %all-gather = f32[16384]{0:T(1024)S(1)} all-gather(f32[2048]{0:T(1024)S(1)} %get-tuple-element.560), channel_id=2, replica_groups=mesh['seq'=8,'ch'=4] {'seq'}, dimensions={0}, use_global_device_ids=true | all-gather | bytes 73728 | tf_op jit(solution)/shard_map/all_gather | solution.py:16
  135.5 1.6 fusion.91
  137.1 1.3 copy-done.2
  138.6 1.8 broadcast_add_fusion
  140.4 2.6 copy.59
  143.0 2.8 all-gather.19.cloned.1.call-done
  145.7 1.8 copy.73
  147.6 2.1 while.54
  149.7 25.4 %while.52 = (s32[]{:T(128)}, f32[8,32,2048]{2,1,0:T(8,128)}, f32[8,32,2048]{2,1,0:T(8,128)}, f32[2048,16]{0,1:T(8,128)S(1)}, f32[2048,16]{0,1:T(8,128)S(1)}, /*index=5*/f32[8,32,16]{1,0,2:T(8,128)S(1)}, s32[]{:T(128)}) while((s32[]{:T(128)}, f32[8,32,2048]{2,1,0:T(8,128)}, f32[8,32,2048]{2,1,0:T(8,128)}, f32[2048,16]{0,1:T(8,128)S(1)}, ...), condition=%wide.region_25.26_spmd, body=%wide.region_23.25_spmd.sunk | while | flops 4194306 | bytes 1845845 | solution.py:177
  150.9 1.4 multiply_reduce_fusion.23
  154.1 1.4 multiply_reduce_fusion.23
  157.2 1.4 multiply_reduce_fusion.23
  160.4 1.4 multiply_reduce_fusion.23
  163.6 1.4 multiply_reduce_fusion.23
  166.7 1.4 multiply_reduce_fusion.23
  169.9 1.4 multiply_reduce_fusion.23
  173.0 1.4 multiply_reduce_fusion.23
  175.1 3.1 fusion.93
  178.2 17.0 %fusion.98 = f32[256,8192]{1,0:T(8,128)} fusion(bf16[256,2048]{1,0:T(8,128)(2,1)S(1)} %fusion.93, bf16[2048,8192]{1,0:T(8,128)(2,1)} %param.30), kind=kOutput, calls=%fused_computation.229 | convolution fusion | flops 8589934592 | bytes 42991616 | tf_op jit(solution)/shard_map/dot_general | solution.py:186
  197.8 67.7 %reduce-scatter.2.cloned.1.call-done = f32[256,2048]{1,0:T(8,128)} async-done(((f32[256,8192]{1,0:T(8,128)}), f32[256,2048]{1,0:T(8,128)}) %reduce-scatter.2.cloned.1.call-update) | async-done | bytes 2097168 | tf_op jit(solution)/shard_map/reduce_scatter | solution.py:187
  265.5 2.0 fusion.87
  267.5 5.8 psum.7
  274.8 117.3 %all-gather.11.cloned.1.call-done = bf16[8192,512]{1,0:T(8,128)(2,1)} async-done(((bf16[1024,512]{1,0:T(8,128)(2,1)}), bf16[8192,512]{1,0:T(8,128)(2,1)}) %all-gather.11.cloned.1.call-update) | async-done | bytes 8388624 | tf_op jit(solution)/shard_map/all_gather | solution.py:38
  392.2 34.7 %all-gather.9.cloned.1.call-done = bf16[256,8192]{1,0:T(8,128)(2,1)} async-done(((bf16[256,2048]{1,0:T(8,128)(2,1)}), bf16[256,8192]{1,0:T(8,128)(2,1)}) %all-gather.9.cloned.1.call-update) | async-done | bytes 4194320 | tf_op jit(solution)/shard_map/all_gather | solution.py:195
  426.8 7.0 convolution_convert_fusion.1
  435.9 39.1 %all-gather.13.cloned.1.call-done = bf16[2048,256]{1,0:T(8,128)(2,1)} async-done(((bf16[256,256]{1,0:T(8,128)(2,1)}), bf16[2048,256]{1,0:T(8,128)(2,1)}) %all-gather.13.cloned.1.call-update) | async-done | bytes 1048592 | tf_op jit(solution)/shard_map/all_gather | solution.py:68
  475.0 1.3 reshape.530
  476.3 40.2 %all-gather.17.cloned.1.call-done = bf16[2048,256]{1,0:T(8,128)(2,1)} async-done(((bf16[256,256]{1,0:T(8,128)(2,1)}), bf16[2048,256]{1,0:T(8,128)(2,1)}) %all-gather.17.cloned.1.call-update) | async-done | bytes 1048592 | tf_op jit(solution)/shard_map/all_gather | solution.py:69
  516.6 2.1 reshape.532
  518.7 635.8 %all-gather.15.cloned.1.call-done = bf16[8192,2048]{1,0:T(8,128)(2,1)} async-done(((bf16[1024,2048]{1,0:T(8,128)(2,1)}), bf16[8192,2048]{1,0:T(8,128)(2,1)}) %all-gather.15.cloned.1.call-update) | async-done | bytes 33554448 | tf_op jit(solution)/shard_map/all_gather | solution.py:37
  1154.5 16.2 %fusion.94 = bf16[32,8,16,128]{3,1,2,0:T(8,128)(2,1)S(1)} fusion(bf16[256,8192]{1,0:T(8,128)(2,1)} %all-gather.9.cloned.1.call-done, bf16[8192,2048]{1,0:T(8,128)(2,1)} %all-gather.15.cloned.1.call-done), kind=kOutput, calls=%fused_computation.216 | convolution fusion | flops 8590458880 | bytes 38797312 | tf_op jit(solution)/shard_map/dot_general | solution.py:42
  1171.3 72.4 %while.55 = (s32[]{:T(128)}, f32[2,8,256]{2,1,0:T(8,128)S(1)}, f32[2,8,256]{2,1,0:T(8,128)S(1)}, f32[2,8,256,128]{3,2,1,0:T(8,128)}, s32[4]{0:T(128)S(1)}, /*ind...) while((s32[]{:T(128)}, f32[2,8,256]{2,1,0:T(8,128)S(1)}, ...), condition=%wide.region_32.33_spmd.clone, body=%wide.region_29.32_spmd.clone.sunk | while | flops 1102729984 | bytes 66328748 | solution.py:100
  1174.0 4.6 fusion.120
  1178.6 4.6 fusion.121
  1184.4 4.0 fusion.123
  1191.2 4.6 fusion.120
  1195.8 4.6 fusion.121
  1201.6 5.2 fusion.123
  1209.6 4.6 fusion.120
  1214.2 4.6 fusion.121
  1220.0 5.2 fusion.123
  1228.0 4.6 fusion.120
  1232.6 4.6 fusion.121
  1238.4 5.2 fusion.123
  1243.7 1.9 fusion.95
  (302 shorter events, 97.7 us)
Async XLA Ops:
  7.2 3.9 copy-start.9
  7.2 4.0 copy-start.8
  7.2 4.8 copy-start.5
  7.2 138.6 %all-gather.19.cloned.1.call-start = ((), (), s32[]{:S(2)}) async-start(), calls=%async_computation.7 | async-start | bytes 1179648 | tf_op jit(solution)/shard_map/all_gather | solution.py:16
  101.9 0.7 copy-start.1
  102.6 162.9 %reduce-scatter.2.cloned.1.call-start = ((), (), s32[]{:S(2)}) async-start(), calls=%async_computation.1 | async-start | bytes 10485760 | tf_op jit(solution)/shard_map/reduce_scatter | solution.py:187
  137.1 1.4 copy-start.2
  149.7 25.5 %copy-start.4 = (bf16[256,2048]{1,0:T(8,128)(2,1)S(1)}, bf16[256,2048]{1,0:T(8,128)(2,1)}, u32[]{:S(2)}) copy-start(bf16[256,2048]{1,0:T(8,128)(2,1)} %param.22) | copy-start | bytes 3145732
  149.7 25.5 %copy-start.7 = (bf16[256,2048]{1,0:T(8,128)(2,1)S(1)}, bf16[256,2048]{1,0:T(8,128)(2,1)}, u32[]{:S(2)}) copy-start(bf16[256,2048]{1,0:T(8,128)(2,1)} %param.23) | copy-start | bytes 3145732
  149.7 25.4 %copy-start.10 = (f32[2048]{0:T(1024)S(1)}, f32[2048]{0:T(1024)}, u32[]{:S(2)}) copy-start(f32[2048]{0:T(1024)} %param.29) | copy-start | bytes 24580
  195.3 196.9 %all-gather.11.cloned.1.call-start = ((), (), s32[]{:S(2)}) async-start(), calls=%async_computation.3 | async-start | bytes 9437184 | tf_op jit(solution)/shard_map/all_gather | solution.py:38
  196.6 1.2 copy-start.11
  196.6 68.9 %copy-start.6 = (bf16[256,2048]{1,0:T(8,128)(2,1)S(1)}, bf16[256,2048]{1,0:T(8,128)(2,1)}, u32[]{:S(2)}) copy-start(bf16[256,2048]{1,0:T(8,128)(2,1)} %param.31) | copy-start | bytes 3145732
  197.7 229.1 %all-gather.9.cloned.1.call-start = ((), (), s32[]{:S(2)}) async-start(), calls=%async_computation.2 | async-start | bytes 5242880 | tf_op jit(solution)/shard_map/all_gather | solution.py:195
  267.5 166.3 %copy-start.3 = (bf16[256,2048]{1,0:T(8,128)(2,1)}, bf16[256,2048]{1,0:T(8,128)(2,1)S(1)}, u32[]{:S(2)}) copy-start(bf16[256,2048]{1,0:T(8,128)(2,1)S(1)} %get-tuple-element.475) | copy-start | bytes 3145732
  274.6 200.4 %all-gather.13.cloned.1.call-start = ((), (), s32[]{:S(2)}) async-start(), calls=%async_computation.4 | async-start | bytes 1179648 | tf_op jit(solution)/shard_map/all_gather | solution.py:68
  434.5 82.0 %all-gather.17.cloned.1.call-start = ((), (), s32[]{:S(2)}) async-start(), calls=%async_computation.6 | async-start | bytes 1179648 | tf_op jit(solution)/shard_map/all_gather | solution.py:69
  435.1 719.4 %all-gather.15.cloned.1.call-start = ((), (), s32[]{:S(2)}) async-start(), calls=%async_computation.5 | async-start | bytes 37748736 | tf_op jit(solution)/shard_map/all_gather | solution.py:37
  1178.6 5.8 copy-start
  1195.8 5.8 copy-start
  1214.2 5.8 copy-start
  1232.6 5.8 copy-start
Sparse Core Ops, SparseCore 0:
  102.7 43.0 all-gather.18
  195.4 70.0 reduce-scatter.1
  267.6 124.4 all-gather.10
  394.2 32.6 all-gather.8
  434.7 40.2 all-gather.12
  477.5 38.9 all-gather.16
  518.1 636.3 all-gather.14
where the time goes:
time: 1260 us; the launch traced here: 1250 us
  waiting for transfers between devices  939 us (75%)
  other arithmetic  113 us (9%)
  matrix products  78.5 us (6%)
  local copies, waits for them, and re-layouts  68.6 us (5%)
  blocking collectives  38.5 us (3%)
  between operations  14.4 us (1%)
    all_gather x1, waiting for transfers between devices, project(): lax.all_gather(query_part, 'seq', axis=0, tiled=True)  636 us
    all_gather x1, waiting for transfers between devices, project(): lax.all_gather(kv_part, 'seq', axis=0, tiled=True)  117 us
    reduce_scatter x1, waiting for transfers between devices, shards(): lax.psum_scatter(partial_terms, 'ch', scatter_dimension=1, tiled=True)  67.7 us
    all_gather x1, waiting for transfers between devices, attend_heads(): lax.all_gather(value_rows, 'seq', axis=0, tiled=True)  40.2 us
    all_gather x1, waiting for transfers between devices, attend_heads(): lax.all_gather(key_rows, 'seq', axis=0, tiled=True)  39.1 us
    all_gather x1, waiting for transfers between devices, shards(): normed = lax.all_gather(normed_local, 'ch', axis=1, tiled=True)  34.7 us
    all_gather x1, blocking collectives, entering_2(): everything = jax.tree.map(lambda part: lax.all_gather(part, axis), array)  32.8 us
    mul x16, other arithmetic, advance_block(): block_steps[position] * block_drive[position]  32.5 us
  transfers between devices with their start and end apart: 7, of which 7 were waited for; matrix products, arithmetic and copies ran while one was open for 1% of the time, Pallas kernels for 0%

commit v1 on v0

v1 whole, which is shorter than its diff:
```python
import math

import jax
import jax.numpy as jnp
from jax import lax
from jax.experimental import pallas as pl
from jax.experimental.pallas import tpu as pltpu
from jax.sharding import PartitionSpec as P


HD = 128
LOG2E = 1.4426950408889634
F32 = jnp.float32
BF16 = jnp.bfloat16
Q_PIECES = 4


def cost(flops, bytes_moved, exps=0):
    return pl.CostEstimate(flops=flops, bytes_accessed=bytes_moved, transcendentals=exps)


def eight(ref, g):
    return ref[pl.ds(pl.multiple_of(g * 8, 8), 8), :]


def rows(block, i, nb):
    return [
        jnp.broadcast_to(block[i : i + 1, j * 128 : (j + 1) * 128], (8, 128)) for j in range(nb)
    ]


def tiles(ref, halves, nb):
    return [
        [ref[h * 8 : h * 8 + 8, j * 128 : j * 128 + 128] for h in range(halves)] for j in range(nb)
    ]


def state_kernel(delta_ref, x_ref, bias_ref, a_ref, b_ref, step_ref, fin_ref, u_ref):
    tokens, lanes = delta_ref.shape
    n = a_ref.shape[0]
    halves, nb = n // 8, lanes // 128
    v = delta_ref[...].astype(F32) + bias_ref[...]
    step = jnp.maximum(v, 0.0) + jnp.log1p(jnp.exp(-jnp.abs(v)))
    step_ref[...] = step
    u_ref[...] = step * x_ref[...].astype(F32)
    fin_ref[n : n + 8, :] = jnp.broadcast_to(jnp.sum(step, axis=0, keepdims=True), (8, lanes))
    a = tiles(a_ref, halves, nb)

    def body(g, carry):
        hs = list(carry)
        step8, u8 = eight(step_ref, g), eight(u_ref, g)
        for i in range(8):
            t = g * 8 + i
            b = [b_ref[pl.ds(pl.multiple_of(t * n + 8 * h, 8), 8), :] for h in range(halves)]
            ds, us = rows(step8, i, nb), rows(u8, i, nb)
            for j in range(nb):
                d, u = ds[j], us[j]
                for h in range(halves):
                    k = j * halves + h
                    hs[k] = jnp.exp2(d * a[j][h]) * hs[k] + u * b[h]
        return tuple(hs)

    zero = jnp.zeros((8, 128), F32)
    hs = lax.fori_loop(0, tokens // 8, body, (zero,) * (halves * nb))
    for j in range(nb):
        for h in range(halves):
            fin_ref[h * 8 : h * 8 + 8, j * 128 : j * 128 + 128] = hs[j * halves + h]


def fold_rows(parts, masks):
    for width, mask in zip((4, 2, 1), masks):
        count = len(parts) // 2
        merged = []
        for i in range(count):
            p, q = parts[i], parts[i + count]
            if width == 4:
                other = pltpu.roll(jnp.where(mask, q, p), 4, 0)
            else:
                other = jnp.where(mask, pltpu.roll(p, 8 - width, 0), pltpu.roll(q, width, 0))
            merged.append(jnp.where(mask, p, q) + other)
        parts = merged
    return parts[0]


def scan_kernel(
    step_ref, x_ref, gate_ref, skip_ref, a_ref, b_ref, c_ref, h_ref, out_ref, u_ref, y_ref
):
    tokens, lanes = step_ref.shape
    n = a_ref.shape[0]
    halves, nb = n // 8, lanes // 128
    u_ref[...] = step_ref[...] * x_ref[...].astype(F32)
    a = tiles(a_ref, halves, nb)
    start = tiles(h_ref, halves, nb)
    sub = lax.broadcasted_iota(jnp.int32, (8, 128), 0)
    masks = [(sub & w) == 0 for w in (4, 2, 1)]

    def body(g, carry):
        hs = list(carry)
        step8, u8 = eight(step_ref, g), eight(u_ref, g)
        sums = [[None] * 8 for _ in range(nb)]
        for i in range(8):
            t = g * 8 + i
            b = [b_ref[pl.ds(pl.multiple_of(t * n + 8 * h, 8), 8), :] for h in range(halves)]
            c = [c_ref[pl.ds(pl.multiple_of(t * n + 8 * h, 8), 8), :] for h in range(halves)]
            ds, us = rows(step8, i, nb), rows(u8, i, nb)
            for j in range(nb):
                d, u = ds[j], us[j]
                total = None
                for h in range(halves):
                    k = j * halves + h
                    hs[k] = jnp.exp2(d * a[j][h]) * hs[k] + u * b[h]
                    term = hs[k] * c[h]
                    total = term if total is None else total + term
                sums[j][i] = total
        for j in range(nb):
            y_ref[pl.ds(pl.multiple_of(g * 8, 8), 8), j * 128 : j * 128 + 128] = fold_rows(sums[j], masks)
        return tuple(hs)

    lax.fori_loop(0, tokens // 8, body, tuple(start[j][h] for j in range(nb) for h in range(halves)))
    x = x_ref[...].astype(F32)
    v = gate_ref[...].astype(F32)
    scanned = y_ref[...] + skip_ref[...] * x
    out_ref[...] = (scanned * (v / (1.0 + jnp.exp(-v)))).astype(BF16)


def scan_specs(tokens, n, lanes):
    wide = pl.BlockSpec((tokens, lanes), lambda i: (0, i))
    one = pl.BlockSpec((1, lanes), lambda i: (0, i))
    state = pl.BlockSpec((n, lanes), lambda i: (0, i))
    whole = pl.BlockSpec((tokens * n, 128), lambda i: (0, 0))
    return wide, one, state, whole


def local_state(delta, x, bias, a2, b_wide):
    tokens, width = delta.shape
    n = a2.shape[0]
    lanes = math.gcd(width, 512)
    wide, one, state, whole = scan_specs(tokens, n, lanes)
    return pl.pallas_call(
        state_kernel,
        grid=(width // lanes,),
        in_specs=[wide, wide, one, state, whole],
        out_specs=[wide, pl.BlockSpec((n + 8, lanes), lambda i: (0, i))],
        out_shape=[
            jax.ShapeDtypeStruct((tokens, width), F32),
            jax.ShapeDtypeStruct((n + 8, width), F32),
        ],
        scratch_shapes=[pltpu.VMEM((tokens, lanes), F32)],
        cost_estimate=cost(8 * tokens * width * n, 8 * tokens * width, tokens * width * n),
        name="local_state",
    )(delta, x, bias, a2, b_wide)


def gated_scan(step, x, gate, skip, a2, b_wide, c_wide, entering):
    tokens, width = step.shape
    n = a2.shape[0]
    lanes = math.gcd(width, 512)
    wide, one, state, whole = scan_specs(tokens, n, lanes)
    return pl.pallas_call(
        scan_kernel,
        grid=(width // lanes,),
        in_specs=[wide, wide, wide, one, state, whole, whole, state],
        out_specs=wide,
        out_shape=jax.ShapeDtypeStruct((tokens, width), BF16),
        scratch_shapes=[pltpu.VMEM((tokens, lanes), F32)] * 2,
        cost_estimate=cost(12 * tokens * width * n, 10 * tokens * width, tokens * width * n),
        name="gated_scan",
    )(step, x, gate, skip, a2, b_wide, c_wide, entering)


def out_kernel(idx_ref, x_ref, w_ref, send_ref, keep_ref):
    prod = jnp.dot(x_ref[...], w_ref[...], preferred_element_type=F32)
    sending = pl.program_id(0) < pl.num_programs(0) // 2

    @pl.when(sending)
    def _():
        send_ref[...] = prod.astype(BF16)

    @pl.when(jnp.logical_not(sending))
    def _():
        keep_ref[...] = prod


def project_blocks(gated, weight, blocks, bn):
    tokens, depth = gated.shape
    count = blocks.shape[0]
    half = count // 2
    return pl.pallas_call(
        out_kernel,
        grid_spec=pltpu.PrefetchScalarGridSpec(
            num_scalar_prefetch=1,
            grid=(count,),
            in_specs=[
                pl.BlockSpec((tokens, depth), lambda j, idx: (0, 0)),
                pl.BlockSpec((depth, bn), lambda j, idx: (0, idx[j])),
            ],
            out_specs=[
                pl.BlockSpec((tokens, bn), lambda j, idx: (0, jnp.minimum(j, half - 1))),
                pl.BlockSpec((tokens, bn), lambda j, idx: (0, jnp.maximum(j - half, 0))),
            ],
        ),
        out_shape=[
            jax.ShapeDtypeStruct((tokens, half * bn), BF16),
            jax.ShapeDtypeStruct((tokens, half * bn), F32),
        ],
        cost_estimate=cost(2 * tokens * depth * count * bn, 2 * depth * count * bn),
    )(blocks, gated, weight)


def qkv_kernel(flag_ref, *refs, groups, tokens):
    xs = refs[: 4 * groups]
    own_w, far_w, send_ref, keep_ref, near_ref, rest_ref = refs[4 * groups :]

    @pl.when(pl.program_id(0) == 0)
    def _():
        swap = flag_ref[0] == 1
        for a in range(groups):
            for half, dst in ((0, near_ref), (1, rest_ref)):
                own = xs[half * 2 * groups + a][...]
                other = xs[half * 2 * groups + groups + a][...]
                dst[a * tokens : (a + 1) * tokens, :] = jnp.where(swap, own, other)
                dst[(groups + a) * tokens : (groups + a + 1) * tokens, :] = jnp.where(
                    swap, other, own
                )

    prod = jnp.dot(near_ref[...], own_w[...], preferred_element_type=F32)
    prod = prod + jnp.dot(rest_ref[...], far_w[...], preferred_element_type=F32)
    half_rows = groups * tokens
    send_ref[...] = prod[:half_rows].astype(BF16)
    keep_ref[...] = prod[half_rows:]


def qkv_piece(flag, xs, own_w, far_w, first, width):
    tokens, rows = xs[0].shape
    groups = len(xs) // 4
    bn = math.gcd(width, 512)
    offset = first // bn
    total = groups * tokens

    def body(*refs):
        qkv_kernel(*refs, groups=groups, tokens=tokens)

    x_spec = pl.BlockSpec((tokens, rows), lambda j, f: (0, 0))
    w_spec = pl.BlockSpec((rows, bn), lambda j, f: (0, offset + j))
    o_spec = pl.BlockSpec((total, bn), lambda j, f: (0, j))
    return pl.pallas_call(
        body,
        grid_spec=pltpu.PrefetchScalarGridSpec(
            num_scalar_prefetch=1,
            grid=(width // bn,),
            in_specs=[x_spec] * len(xs) + [w_spec, w_spec],
            out_specs=[o_spec, o_spec],
            scratch_shapes=[pltpu.VMEM((2 * total, rows), BF16)] * 2,
        ),
        out_shape=[
            jax.ShapeDtypeStruct((total, width), BF16),
            jax.ShapeDtypeStruct((total, width), F32),
        ],
        cost_estimate=cost(8 * total * rows * width, 4 * rows * width + 6 * total * width),
    )(flag, *xs, own_w, far_w)


def dot_t(q, k):
    return lax.dot_general(q, k, (((1,), (1,)), ((), ())), preferred_element_type=F32)


def lane_tiles(v, op):
    out = v[:, :128]
    for i in range(1, v.shape[1] // 128):
        out = op(out, v[:, i * 128 : i * 128 + 128])
    return out


def attn_kernel(pos_ref, q_ref, k_ref, v_ref, k2_ref, v2_ref, *rest):
    o_ref, s_ref = rest[-2:]
    tokens = q_ref.shape[0]
    depth = k_ref.shape[0]
    scale = LOG2E / math.sqrt(HD)
    z, y = pos_ref[0], pos_ref[1]
    q = q_ref[...]
    r = lax.broadcasted_iota(jnp.int32, (tokens, tokens), 0)
    c = lax.broadcasted_iota(jnp.int32, (tokens, tokens), 1)
    blocks = []
    for j in range(depth):
        blocks.append((k_ref, v_ref, j, None if j == 0 else j <= z))
        blocks.append((k2_ref, v2_ref, j, y == 1 if j == 0 else j <= z))
    top = None
    for i, (keys, _, j, valid) in enumerate(blocks):
        s = dot_t(q, keys[j])
        if valid is None:
            s = jnp.where(c <= r, s, -1e30)
        s_ref[i] = s
        m = lane_tiles(s, jnp.maximum)
        if valid is not None:
            m = jnp.where(valid, m, -1e30)
        top = m if top is None else jnp.maximum(top, m)
    top = jnp.max(top, axis=1, keepdims=True) * scale
    total, acc = None, None
    for i, (_, vals, j, valid) in enumerate(blocks):
        shift = top if valid is None else top + jnp.where(valid, 0.0, 1e30)
        p = jnp.exp2(s_ref[i] * scale - shift)
        part = lane_tiles(p, jnp.add)
        prod = jnp.dot(p.astype(BF16), vals[j], preferred_element_type=F32)
        total = part if total is None else total + part
        acc = prod if acc is None else acc + prod
    o_ref[...] = (acc / jnp.sum(total, axis=1, keepdims=True)).astype(BF16)


def attend(pos, q, near_kv, far_kv, done, first_head, all_heads, kv_heads):
    tokens, width = q.shape
    heads = width // HD
    depth = near_kv.shape[0]

    def kv(h):
        return (first_head + h) * kv_heads // all_heads

    q_spec = pl.BlockSpec((tokens, HD), lambda h, p: (0, h))
    o_spec = pl.BlockSpec((tokens, HD), lambda h, p: (0, first_head + h))
    extra = [] if done is None else [done]
    k_spec = pl.BlockSpec((depth, tokens, HD), lambda h, p: (0, 0, kv(h)))
    v_spec = pl.BlockSpec((depth, tokens, HD), lambda h, p: (0, 0, kv_heads + kv(h)))
    return pl.pallas_call(
        attn_kernel,
        grid_spec=pltpu.PrefetchScalarGridSpec(
            num_scalar_prefetch=1,
            grid=(heads,),
            in_specs=[q_spec, k_spec, v_spec, k_spec, v_spec]
            + [pl.BlockSpec(memory_space=pl.ANY)] * len(extra),
            out_specs=o_spec,
            scratch_shapes=[pltpu.VMEM((2 * depth, tokens, tokens), F32)],
        ),
        out_shape=jax.ShapeDtypeStruct((tokens, all_heads * HD), BF16),
        input_output_aliases={6: 0} if extra else {},
        cost_estimate=cost(
            8 * tokens * tokens * depth * width, 4 * tokens * width, 2 * tokens * tokens * depth * heads
        ),
    )(pos, q, near_kv, near_kv, far_kv, far_kv, *extra)


def shards(
    mamba_in,
    gate_in,
    delta_in,
    step_bias,
    decay_log,
    input_map_state,
    state_out,
    skip_gain,
    out_weight,
    residual,
    norm_gain,
    query_weight,
    key_weight,
    value_weight,
):
    S, C = lax.axis_size("seq"), lax.axis_size("ch")
    s, c = lax.axis_index("seq"), lax.axis_index("ch")
    Z, G = S // 2, S // 4
    z, y, k = s // 2, s % 2, c % 2
    tokens, width = mamba_in.shape
    n = decay_log.shape[1]
    model = out_weight.shape[1]
    R = model // S

    def swap_y(v):
        return lax.ppermute(v, "seq", [(i, i ^ 1) for i in range(S)])

    def xor_z(v, d):
        return lax.ppermute(v, "seq", [(i, i ^ (2 * d)) for i in range(S)])

    def xor_c(v, d):
        return lax.ppermute(v, "ch", [(i, i ^ d) for i in range(C)])

    a2 = (-LOG2E) * jnp.exp(decay_log).T
    b_wide = jnp.broadcast_to(input_map_state.astype(F32).reshape(-1, 1), (tokens * n, 128))
    c_wide = jnp.broadcast_to(state_out.astype(F32).reshape(-1, 1), (tokens * n, 128))

    gain = lax.dynamic_update_slice_in_dim(jnp.zeros((model,), BF16), norm_gain, c * width, 0)
    d = 1
    while d < C:
        gain = gain + xor_c(gain, d)
        d *= 2
    gain = gain.astype(F32)

    step, final = local_state(delta_in, mamba_in, step_bias[None], a2, b_wide)

    def pack(f, t):
        high = t.astype(BF16)
        low = (t - high.astype(F32)).astype(BF16)
        wide = [v.reshape(n, width // n) for v in (high, low)]
        return jnp.concatenate([f.astype(BF16)] + wide, axis=1)

    def unpack(v):
        part = width // n
        high, low = v[:, width : width + part], v[:, width + part :]
        return v[:, :width].astype(F32), (high.astype(F32) + low.astype(F32)).reshape(1, width)

    f_own, t_own = final[:n], final[n : n + 1]
    pair = swap_y(pack(f_own, t_own))
    f_far, t_far = unpack(pair)
    lead = y == 0
    f_pair = jnp.where(lead, f_own, f_far) * jnp.exp2(
        jnp.where(lead, t_far, t_own) * a2
    ) + jnp.where(lead, f_far, f_own)
    both = pack(f_pair, t_own + t_far)
    earlier = []
    for j in range(1, Z):
        earlier.append(lax.ppermute(both, "seq", [(i, i + 2 * j) for i in range(S - 2 * j)]))
    entering = unpack(earlier[-1])[0]
    for e in earlier[-2::-1]:
        f, t = unpack(e)
        entering = entering * jnp.exp2(t * a2) + f
    entering = jnp.where(lead, entering, entering * jnp.exp2(t_far * a2) + f_far)

    q_heads = query_weight.shape[1] // HD
    all_heads = query_weight.shape[1] * C // HD
    group = all_heads // (key_weight.shape[1] // HD)
    kv_heads = max(1, q_heads // group)
    first = (c * q_heads // group) * HD
    kv_own = jnp.concatenate(
        [lax.dynamic_slice_in_dim(w, first, kv_heads * HD, 1) for w in (key_weight, value_weight)],
        axis=1,
    )
    kv_far = swap_y(kv_own)
    q_far = swap_y(query_weight)

    gated = gated_scan(
        step, mamba_in, gate_in, skip_gain[None], a2, b_wide, c_wide, entering
    )

    def move(blocks):
        own = []
        for a in range(G):
            perm = []
            for zi in range(Z):
                for yi in range(2):
                    for ci in range(C):
                        zo = 2 * ((zi // 2) ^ a) + ci % 2
                        perm.append(
                            ((2 * zi + yi) * C + ci, (2 * zo + yi) * C + ci - ci % 2 + zi % 2)
                        )
            own.append(lax.ppermute(blocks[a], ("seq", "ch"), perm))
        return own + [xor_c(v, 1) for v in own]

    moved = []
    if C == Z and G == 2:
        cx = c // 2
        bn = math.gcd(R, 1024)
        per = R // bn
        straight = cx == z // 2
        sums, mixed = jnp.zeros((tokens,), F32), []
        for half in (0, 1):
            side = y ^ half
            places = jnp.stack([cx, cx ^ 1])
            m = 2 * (2 * places[None, :] + jnp.stack([1 - k, k])[:, None]) + side
            ids = m[..., None] * per + jnp.arange(per, dtype=jnp.int32)
            send, keep = project_blocks(gated, out_weight, ids.reshape(-1).astype(jnp.int32), bn)
            if half:
                keep, *mixed = lax.optimization_barrier((keep, *mixed))
            total = keep + xor_c(send, 1).astype(F32)
            got = xor_c(total[:, R:].astype(BF16), 2)
            if half:
                got, _ = lax.optimization_barrier((got, scaled))
            rest = lax.dynamic_slice_in_dim(residual, side * R, R, 1).astype(F32)
            own = (total[:, :R] + got.astype(F32) + rest).astype(BF16)
            other = xor_c(own, 2)
            mixed.append(own)
            scaled = []
            for e, v in enumerate((own, other)):
                first_col = (2 * (2 * places[e] + k) + side) * R
                wide = v.astype(F32)
                sums = sums + jnp.sum(wide * wide, axis=1)
                g = lax.dynamic_slice_in_dim(gain, first_col, R, 0)
                scaled.append((wide * g[None]).astype(BF16))
            moved += move(
                [
                    jnp.where(straight, scaled[0], scaled[1]),
                    jnp.where(straight, scaled[1], scaled[0]),
                ],
            )
        sums = sums + xor_c(sums, 1)
        mamba_out = jnp.concatenate(
            [jnp.where(y == i, mixed[0], mixed[1]) for i in (0, 1)], axis=1
        )
    else:
        partial_terms = jnp.dot(gated, out_weight, preferred_element_type=F32)
        projected = lax.psum_scatter(partial_terms, "ch", scatter_dimension=1, tiled=True)
        mamba_out = (residual.astype(F32) + projected).astype(BF16)
        full = lax.all_gather(mamba_out, "ch", axis=1, tiled=True).astype(F32)
        sums = jnp.sum(full * full, axis=1)
        full = (full * gain[None]).astype(BF16)
        for half in (0, 1):
            cols = [(2 * (2 * ((z // 2) ^ a) + k) + (y ^ half)) * R for a in range(G)]
            moved += move([lax.dynamic_slice_in_dim(full, v, R, 1) for v in cols])
    inverse = lax.rsqrt(sums / model + 1e-06)[:, None]

    flag = ((k ^ (z % 2)).astype(jnp.int32))[None]

    def project(own_w, far_w, lo, size, last=None):
        send, keep = qkv_piece(flag, moved, own_w, far_w, lo, size)
        got = xor_z(send, 1)
        if last is not None:
            got, _ = lax.optimization_barrier((got, last[0]))
        got = got.astype(F32)
        parts = [
            keep[a * tokens : (a + 1) * tokens] + got[a * tokens : (a + 1) * tokens]
            for a in range(G)
        ]
        bit = G // 2
        while bit:
            out = jnp.concatenate([v.astype(BF16) for v in parts[bit:]], axis=0)
            got = xor_z(out, 2 * bit)
            if last is not None:
                got, _ = lax.optimization_barrier((got, last[1]))
            got = got.astype(F32)
            parts = [parts[i] + got[i * tokens : (i + 1) * tokens] for i in range(bit)]
            bit //= 2
        return out, (parts[0] * inverse).astype(BF16)

    last = project(kv_own, kv_far, 0, kv_own.shape[1])
    kv_rows = last[1]
    near, far = [kv_rows], []
    for _ in range(1, Z):
        near.append(lax.ppermute(near[-1], "seq", [(i, i + 2) for i in range(S - 2)]))
    for v in near:
        far.append(swap_y(v))
    near, far = jnp.stack(near), jnp.stack(far)
    pos = jnp.stack([z, y]).astype(jnp.int32)
    result = None
    q_width = query_weight.shape[1]
    pieces = math.gcd(Q_PIECES, q_width // HD)
    size = q_width // pieces
    for i in range(pieces):
        last = project(query_weight, q_far, i * size, size, last)
        q = last[1]
        result = attend(pos, q, near, far, result, i * size // HD, q_heads, kv_heads)
    return (mamba_out, result)


def solution(mesh):
    return jax.shard_map(
        shards,
        mesh=mesh,
        in_specs=(
            P("seq", "ch"),
            P("seq", "ch"),
            P("seq", "ch"),
            P("ch"),
            P("ch", None),
            P("seq", None),
            P("seq", None),
            P("ch"),
            P("ch", None),
            P("seq", "ch"),
            P("ch"),
            P("seq", "ch"),
            P("seq", None),
            P("seq", None),
        ),
        out_specs=(P("seq", "ch"), P("seq", "ch")),
        check_vma=False,
    )
```

time: 1260 us -> 353 us (0.28)
  waiting for transfers between devices: 939 us -> 121 us
  Pallas kernels: 0 us -> 108 us
  other arithmetic: 113 us -> 30.4 us
  starting transfers between devices: 0.51 us -> 80.9 us
  matrix products: 78.5 us -> 0 us
  local copies, waits for them, and re-layouts: 68.6 us -> 10.5 us
  blocking collectives: 38.5 us -> 0 us
  between operations: 14.4 us -> 1.13 us
    all_gather x6 -> x0, waiting for transfers between devices: 870 us -> none  [the longest x1 636 us: project(): lax.all_gather(query_part, 'seq', axis=0, tiled=True)]
    ppermute x0 -> x40, waiting for transfers between devices: none -> 121 us  [the longest x13 32.6 us: xor_c(): return lax.ppermute(v, 'ch', [(i, i ^ d) for i in range(C)])]
    pallas_call x0 -> x13, Pallas kernels: none -> 108 us  [the longest x5 31 us: qkv_piece(): pl.pallas_call(body, grid_spec=pltpu.PrefetchScalarGridSpec(num_scalar_pr...]
    ppermute x0 -> x40, starting transfers between devices: none -> 80.9 us  [the longest x3 24.5 us: shards(): lax.ppermute(near[-1], 'seq', [(i, i + 2) for i in range(S - 2)])]
    dot_general x11 -> x0, matrix products: 78.5 us -> none  [the longest x4 19.7 us: one_block(): jnp.einsum('kgts,skd->kgtd', weights.astype(jnp.bfloat16), value_block, p...]
    reduce_scatter x1 -> x0, waiting for transfers between devices: 67.7 us -> none  [shards(): lax.psum_scatter(partial_terms, 'ch', scatter_dimension=1, tiled=True)]
    reduce_sum x94 -> x4, other arithmetic: 55.2 us -> 3.25 us  [shards(): sums = sums + jnp.sum(wide * wide, axis=1)]
    all_gather x1 -> x0, blocking collectives: 32.8 us -> none  [entering_2(): everything = jax.tree.map(lambda part: lax.all_gather(part, axis), array)]
  transfers between devices with their start and end apart: 7 -> 40, of which waited for: 7 -> 18; matrix products, arithmetic and copies ran while one was open for 1% -> 7% of each run, Pallas kernels for 0% -> 12%
where the time goes in v1:
time: 353 us; the launch traced here: 352 us
  waiting for transfers between devices  121 us (34%)
  Pallas kernels  108 us (31%)
  starting transfers between devices  80.9 us (23%)
  other arithmetic  30.4 us (9%)
  local copies, waits for them, and re-layouts  10.5 us (3%)
    ppermute x13, waiting for transfers between devices, xor_c(): return lax.ppermute(v, 'ch', [(i, i ^ d) for i in range(C)])  32.6 us
    ppermute x10, waiting for transfers between devices, xor_z(): return lax.ppermute(v, 'seq', [(i, i ^ 2 * d) for i in range(S)])  31.9 us
    pallas_call x5, Pallas kernels, qkv_piece(): pl.pallas_call(body, grid_spec=pltpu.PrefetchScalarGridSpec(num_scalar_pr...  31 us
    ppermute x4, waiting for transfers between devices, move(): own.append(lax.ppermute(blocks[a], ('seq', 'ch'), perm))  30.2 us
    pallas_call x4, Pallas kernels, attend(): pl.pallas_call(attn_kernel, grid_spec=pltpu.PrefetchScalarGridSpec(num_sc...  28.7 us
    ppermute x3, starting transfers between devices, shards(): lax.ppermute(near[-1], 'seq', [(i, i + 2) for i in range(S - 2)])  24.5 us
    ppermute x7, waiting for transfers between devices, swap_y(): return lax.ppermute(v, 'seq', [(i, i ^ 1) for i in range(S)])  22.8 us
    pallas_call x2, Pallas kernels, project_blocks(): pl.pallas_call(out_kernel, grid_spec=pltpu.PrefetchScalarGridSpec(num_sca...  21.9 us
  transfers between devices with their start and end apart: 40, of which 18 were waited for; matrix products, arithmetic and copies ran while one was open for 7% of the time, Pallas kernels for 12%

profile of v1, /device:TPU:0, one launch (start us, length us, event | category | flops | bytes accessed | tf_op | source)
XLA Modules:
  0.0 351.7 jit_solution(11590120193008817607)
XLA Ops:
  1.5 1.6 multiply_bitcast_fusion.a_ref
  3.1 1.9 broadcast_in_dim.44.b_ref
  5.1 10.8 %local_state.1 = (f32[256,2048]{1,0:T(8,128)}, f32[24,2048]{1,0:T(8,128)}) custom-call(bf16[256,2048]{1,0:T(8,128)(2,1)} %delta_ref.1, bf16[256,2048]{1,0:T(8,128)(2,1)} %x_ref.3, f32[1,2048]{1,0:T(1,128)} %bitcast.64, f32[16,2048]{1,0:T(8,128)} %multiply_bitcast_fusion.a_ref, f32[4096,128]{1,0:T(8,128)} %broadcast_in_dim.44.b_ref), custom_call_target="tpu_custom_call" | custom-call | flops 67108864 | bytes 4194304 | tf_op jit(solution)/shard_map/local_state/pallas_call | solution.py:139
  17.6 3.1 collective-permute-start
  20.8 2.3 collective-permute-done
  25.8 4.0 %collective-permute-start.3 = (bf16[16,2304]{1,0:T(8,128)(2,1)S(1)}, bf16[16,2304]{1,0:T(8,128)(2,1)S(1)}, u32[]{:S(2)}, u32[]{:S(2)}) collective-permute-start(bf16[16,2304]{1,0:T(8,128)(2,1)S(1)} %pad_maximum_fusion.5), channel_id=1, source_target_pairs={{0,8},{4,12},{8,16},{12,20},{16,24},{20,28},{1,9},{5,13},{9,17},{1... | collective-permute-start | bytes 221192 | tf_op jit(solution)/shard_map/ppermute | solution.py:408
  30.6 4.5 %collective-permute-start.2 = (bf16[16,2304]{1,0:T(8,128)(2,1)S(1)}, bf16[16,2304]{1,0:T(8,128)(2,1)S(1)}, u32[]{:S(2)}, u32[]{:S(2)}) collective-permute-start(bf16[16,2304]{1,0:T(8,128)(2,1)S(1)} %pad_maximum_fusion.5), channel_id=1, source_target_pairs={{0,16},{4,20},{8,24},{12,28},{1,17},{5,21},{9,25},{13,29},{2,18},{... | collective-permute-start | bytes 221192 | tf_op jit(solution)/shard_map/ppermute | solution.py:408
  37.1 1.3 collective-permute-done.1
  39.2 2.0 broadcast_in_dim.48.c_ref
  41.1 15.8 %gated_scan.1.x_ref = bf16[256,2048]{1,0:T(8,128)(2,1)} custom-call(f32[256,2048]{1,0:T(8,128)} %get-tuple-element.29.step_ref, bf16[256,2048]{1,0:T(8,128)(2,1)} %x_ref.3, bf16[256,2048]{1,0:T(8,128)(2,1)} %gate_ref.1, f32[1,2048]{1,0:T(1,128)} %bitcast.65, f32[16,2048]{1,0:T(8,128)} %multiply_bitcast_fusion.a_ref, f32[4096,128]{1,0:T(8,128)} %broadcast_in_dim.44.b_ref, ...), custom_call_target="tpu_custom_call" | custom-call | flops 100663296 | bytes 5242880 | tf_op jit(solution)/shard_map/gated_scan/pallas_call | solution.py:159
  56.9 10.9 %shard_map.150 = (bf16[256,2048]{1,0:T(8,128)(2,1)}, f32[256,2048]{1,0:T(8,128)}) custom-call(s32[4]{0:T(128)} %add.232.idx_ref, bf16[256,2048]{1,0:T(8,128)(2,1)} %gated_scan.1.x_ref, bf16[2048,8192]{1,0:T(8,128)(2,1)} %w_ref.3), custom_call_target="tpu_custom_call" | custom-call | flops 4294967296 | bytes 16777216 | tf_op jit(solution)/shard_map/pallas_call | solution.py:188
  68.4 11.0 %shard_map.149 = (bf16[256,2048]{1,0:T(8,128)(2,1)}, f32[256,2048]{1,0:T(8,128)}) custom-call(s32[4]{0:T(128)} %add.221.idx_ref, bf16[256,2048]{1,0:T(8,128)(2,1)} %gated_scan.1.x_ref, bf16[2048,8192]{1,0:T(8,128)(2,1)} %w_ref.3), custom_call_target="tpu_custom_call" | custom-call | flops 4294967296 | bytes 16777216 | tf_op jit(solution)/shard_map/pallas_call | solution.py:188
  79.9 1.9 convert_add_fusion.1
  81.9 1.6 collective-permute-start.5
  86.1 1.5 collective-permute-start.25
  88.7 7.2 %collective-permute-done.5 = bf16[256,1024]{1,0:T(8,128)(2,1)S(1)} collective-permute-done((bf16[256,1024]{1,0:T(8,128)(2,1)S(1)}, bf16[256,1024]{1,0:T(8,128)(2,1)S(1)}, u32[]{:S(2)}, u32[]{:S(2)}) %collective-permute-start.5) | collective-permute-done | bytes 524320 | tf_op jit(solution)/shard_map/ppermute | solution.py:372
  95.9 1.3 fusion.1
  97.3 1.6 collective-permute-start.10
  98.8 1.6 convert_add_fusion
  101.2 11.0 %collective-permute-done.10 = bf16[256,1024]{1,0:T(8,128)(2,1)S(1)} collective-permute-done((bf16[256,1024]{1,0:T(8,128)(2,1)S(1)}, bf16[256,1024]{1,0:T(8,128)(2,1)S(1)}, u32[]{:S(2)}, u32[]{:S(2)}) %collective-permute-start.10) | collective-permute-done | bytes 524320 | tf_op jit(solution)/shard_map/ppermute | solution.py:372
  113.3 8.2 %collective-permute-done.7 = bf16[256,1024]{1,0:T(8,128)(2,1)S(1)} collective-permute-done((bf16[256,1024]{1,0:T(8,128)(2,1)S(1)}, bf16[256,1024]{1,0:T(8,128)(2,1)S(1)}, u32[]{:S(2)}, u32[]{:S(2)}) %collective-permute-start.7) | collective-permute-done | bytes 524320 | tf_op jit(solution)/shard_map/ppermute | solution.py:372
  121.8 1.6 collective-permute-start.15
  124.2 1.7 collective-permute-start.11
  125.9 2.0 collective-permute-start.12
  127.9 6.1 %collective-permute-done.15 = bf16[256,1024]{1,0:T(8,128)(2,1)S(1)} collective-permute-done((bf16[256,1024]{1,0:T(8,128)(2,1)S(1)}, bf16[256,1024]{1,0:T(8,128)(2,1)S(1)}, u32[]{:S(2)}, u32[]{:S(2)}) %collective-permute-start.15) | collective-permute-done | bytes 524320 | tf_op jit(solution)/shard_map/ppermute | solution.py:372
  134.0 1.9 broadcast_select_fusion
  135.9 1.7 collective-permute-start.16
  137.6 2.0 collective-permute-start.17
  140.4 2.9 collective-permute-start.13
  143.3 13.9 %collective-permute-done.12.refs_2_ = bf16[256,1024]{1,0:T(8,128)(2,1)S(1)} collective-permute-done((bf16[256,1024]{1,0:T(8,128)(2,1)}, bf16[256,1024]{1,0:T(8,128)(2,1)S(1)}, u32[]{:S(2)}, u32[]{:S(2)}) %collective-permute-start.12) | collective-permute-done | bytes 524320 | tf_op jit(solution)/shard_map/ppermute | solution.py:442
  157.7 16.3 %collective-permute-done.17.refs_6_ = bf16[256,1024]{1,0:T(8,128)(2,1)S(1)} collective-permute-done((bf16[256,1024]{1,0:T(8,128)(2,1)}, bf16[256,1024]{1,0:T(8,128)(2,1)S(1)}, u32[]{:S(2)}, u32[]{:S(2)}) %collective-permute-start.17) | collective-permute-done | bytes 524320 | tf_op jit(solution)/shard_map/ppermute | solution.py:442
  174.0 1.4 fusion.7
  175.5 2.3 pad_maximum_fusion
  179.8 6.2 %shard_map.155 = (bf16[512,512]{1,0:T(8,128)(2,1)}, f32[512,512]{1,0:T(8,128)}) custom-call(s32[1]{0:T(128)} %bitcast.18.refs_0_, bf16[256,1024]{1,0:T(8,128)(2,1)} %copy-done, bf16[256,1024]{1,0:T(8,128)(2,1)} %copy-done.1, bf16[256,1024]{1,0:T(8,128)(2,1)} %copy-done.4, bf16[256,1024]{1,0:T(8,128)(2,1)} %copy-done.5, bf16[256,1024]{1,0:T(8,128)(2,1)} %copy-done.2, ...), custom_call_target="tpu_custom_call" | custom-call | flops 2147483648 | bytes 3670016 | tf_op jit(solution)/shard_map/pallas_call | solution.py:246
  186.7 15.1 %collective-permute-done.20.refs_10_ = bf16[1024,2048]{1,0:T(8,128)(2,1)} collective-permute-done((bf16[1024,2048]{1,0:T(8,128)(2,1)}, bf16[1024,2048]{1,0:T(8,128)(2,1)}, u32[]{:S(2)}, u32[]{:S(2)}) %collective-permute-start.20) | collective-permute-done | bytes 4194336 | tf_op jit(solution)/shard_map/ppermute | solution.py:366
  201.8 6.2 %shard_map.154 = (bf16[512,512]{1,0:T(8,128)(2,1)}, f32[512,512]{1,0:T(8,128)}) custom-call(s32[1]{0:T(128)} %bitcast.18.refs_0_, bf16[256,1024]{1,0:T(8,128)(2,1)} %copy-done, bf16[256,1024]{1,0:T(8,128)(2,1)} %copy-done.1, bf16[256,1024]{1,0:T(8,128)(2,1)} %copy-done.4, bf16[256,1024]{1,0:T(8,128)(2,1)} %copy-done.5, bf16[256,1024]{1,0:T(8,128)(2,1)} %copy-done.2, ...), custom_call_target="tpu_custom_call" | custom-call | flops 2147483648 | bytes 3670016 | tf_op jit(solution)/shard_map/pallas_call | solution.py:246
  208.0 6.3 %shard_map.153 = (bf16[512,512]{1,0:T(8,128)(2,1)}, f32[512,512]{1,0:T(8,128)}) custom-call(s32[1]{0:T(128)} %bitcast.18.refs_0_, bf16[256,1024]{1,0:T(8,128)(2,1)} %copy-done, bf16[256,1024]{1,0:T(8,128)(2,1)} %copy-done.1, bf16[256,1024]{1,0:T(8,128)(2,1)} %copy-done.4, bf16[256,1024]{1,0:T(8,128)(2,1)} %copy-done.5, bf16[256,1024]{1,0:T(8,128)(2,1)} %copy-done.2, ...), custom_call_target="tpu_custom_call" | custom-call | flops 2147483648 | bytes 3670016 | tf_op jit(solution)/shard_map/pallas_call | solution.py:246
  214.3 1.9 collective-permute-start.23
  217.5 2.9 collective-permute-start.31
  220.4 6.2 %shard_map.152 = (bf16[512,512]{1,0:T(8,128)(2,1)}, f32[512,512]{1,0:T(8,128)}) custom-call(s32[1]{0:T(128)} %bitcast.18.refs_0_, bf16[256,1024]{1,0:T(8,128)(2,1)} %copy-done, bf16[256,1024]{1,0:T(8,128)(2,1)} %copy-done.1, bf16[256,1024]{1,0:T(8,128)(2,1)} %copy-done.4, bf16[256,1024]{1,0:T(8,128)(2,1)} %copy-done.5, bf16[256,1024]{1,0:T(8,128)(2,1)} %copy-done.2, ...), custom_call_target="tpu_custom_call" | custom-call | flops 2147483648 | bytes 3670016 | tf_op jit(solution)/shard_map/pallas_call | solution.py:246
  226.5 1.9 collective-permute-start.22
  228.5 6.2 %shard_map.151 = (bf16[512,512]{1,0:T(8,128)(2,1)}, f32[512,512]{1,0:T(8,128)}) custom-call(s32[1]{0:T(128)} %bitcast.18.refs_0_, bf16[256,1024]{1,0:T(8,128)(2,1)} %copy-done, bf16[256,1024]{1,0:T(8,128)(2,1)} %copy-done.1, bf16[256,1024]{1,0:T(8,128)(2,1)} %copy-done.4, bf16[256,1024]{1,0:T(8,128)(2,1)} %copy-done.5, bf16[256,1024]{1,0:T(8,128)(2,1)} %copy-done.2, ...), custom_call_target="tpu_custom_call" | custom-call | flops 2147483648 | bytes 3670016 | tf_op jit(solution)/shard_map/pallas_call | solution.py:246
  234.7 2.7 collective-permute-done.31
  238.5 7.3 %collective-permute-start.33 = (bf16[256,512]{1,0:T(8,128)(2,1)S(1)}, bf16[256,512]{1,0:T(8,128)(2,1)S(1)}, u32[]{:S(2)}, u32[]{:S(2)}) collective-permute-start(bf16[256,512]{1,0:T(8,128)(2,1)S(1)} %fusion.14), channel_id=1, source_target_pairs={{0,8},{4,12},{8,16},{12,20},{16,24},{20,28},{1,9},{5,13},{9,17},{1... | collective-permute-start | bytes 786440 | tf_op jit(solution)/shard_map/ppermute | solution.py:524
  245.8 1.6 collective-permute-start.36
  248.0 11.6 %collective-permute-done.22 = bf16[512,512]{1,0:T(8,128)(2,1)} collective-permute-done((bf16[512,512]{1,0:T(8,128)(2,1)}, bf16[512,512]{1,0:T(8,128)(2,1)}, u32[]{:S(2)}, u32[]{:S(2)}) %collective-permute-start.22) | collective-permute-done | bytes 524320 | tf_op jit(solution)/shard_map/ppermute | solution.py:369
  259.6 2.3 collective-permute-start.29
  263.2 6.5 %collective-permute-done.21 = bf16[512,512]{1,0:T(8,128)(2,1)S(1)} collective-permute-done((bf16[512,512]{1,0:T(8,128)(2,1)}, bf16[512,512]{1,0:T(8,128)(2,1)S(1)}, u32[]{:S(2)}, u32[]{:S(2)}) %collective-permute-start.21) | collective-permute-done | bytes 524320 | tf_op jit(solution)/shard_map/ppermute | solution.py:369
  269.7 4.3 %collective-permute-start.28 = (bf16[256,512]{1,0:T(8,128)(2,1)S(1)}, bf16[256,512]{1,0:T(8,128)(2,1)S(1)}, u32[]{:S(2)}, u32[]{:S(2)}) collective-permute-start(bf16[256,512]{1,0:T(8,128)(2,1)S(1)} %fusion.28), channel_id=1, source_target_pairs={{0,16},{4,20},{8,24},{12,28},{16,0},{20,4},{24,8},{28,12},{1,17},{... | collective-permute-start | bytes 786440 | tf_op jit(solution)/shard_map/ppermute | solution.py:369
  274.2 3.9 %collective-permute-start.27 = (bf16[256,512]{1,0:T(8,128)(2,1)S(1)}, bf16[256,512]{1,0:T(8,128)(2,1)S(1)}, u32[]{:S(2)}, u32[]{:S(2)}) collective-permute-start(bf16[256,512]{1,0:T(8,128)(2,1)S(1)} %fusion.24), channel_id=1, source_target_pairs={{0,16},{4,20},{8,24},{12,28},{16,0},{20,4},{24,8},{28,12},{1,17},{... | collective-permute-start | bytes 786440 | tf_op jit(solution)/shard_map/ppermute | solution.py:369
  278.1 4.4 %collective-permute-start.34 = (bf16[256,512]{1,0:T(8,128)(2,1)S(1)}, bf16[256,512]{1,0:T(8,128)(2,1)S(1)}, u32[]{:S(2)}, u32[]{:S(2)}) collective-permute-start(bf16[256,512]{1,0:T(8,128)(2,1)S(1)} %collective-permute-done.33), channel_id=1, source_target_pairs={{0,8},{4,12},{8,16},{12,20},{16,24},{20,28},{1,9},{5,13},{9,17},{1... | collective-permute-start | bytes 786440 | tf_op jit(solution)/shard_map/ppermute | solution.py:524
  283.3 7.7 %collective-permute-done.29 = bf16[256,512]{1,0:T(8,128)(2,1)S(1)} collective-permute-done((bf16[256,512]{1,0:T(8,128)(2,1)S(1)}, bf16[256,512]{1,0:T(8,128)(2,1)S(1)}, u32[]{:S(2)}, u32[]{:S(2)}) %collective-permute-start.29) | collective-permute-done | bytes 262176 | tf_op jit(solution)/shard_map/ppermute | solution.py:369
  291.0 1.5 collective-permute-start.37
  293.3 3.3 collective-permute-done.28
  296.6 12.8 %collective-permute-start.35 = (bf16[256,512]{1,0:T(8,128)(2,1)S(1)}, bf16[256,512]{1,0:T(8,128)(2,1)S(1)}, u32[]{:S(2)}, u32[]{:S(2)}) collective-permute-start(bf16[256,512]{1,0:T(8,128)(2,1)S(1)} %collective-permute-done.34), channel_id=1, source_target_pairs={{0,8},{4,12},{8,16},{12,20},{16,24},{20,28},{1,9},{5,13},{9,17},{1... | collective-permute-start | bytes 786440 | tf_op jit(solution)/shard_map/ppermute | solution.py:524
  310.2 1.5 collective-permute-start.38
  311.7 1.3 collective-permute-done.35
  313.0 1.5 collective-permute-start.39
  316.5 2.6 collective-permute-done.38
  319.1 2.8 collective-permute-done.39
  323.0 7.1 %shard_map.156.rest_0_ = bf16[256,2048]{1,0:T(8,128)(2,1)} custom-call(s32[2]{0:T(128)} %pad_add_fusion.1.pos_ref, bf16[256,512]{1,0:T(8,128)(2,1)} %fusion.17.q_ref, bf16[4,256,512]{2,1,0:T(8,128)(2,1)} %pad_maximum_fusion.2.k_ref.v_ref, bf16[4,256,512]{2,1,0:T(8,128)(2,1)} %pad_maximum_fusion.2.k_ref.v_ref, ...), custom_call_target="tpu_custom_call" | custom-call | flops 1073741824 | bytes 524288 | tf_op jit(solution)/shard_map/pallas_call | solution.py:322
  330.2 7.2 %shard_map.157.rest_0_ = bf16[256,2048]{1,0:T(8,128)(2,1)} custom-call(s32[2]{0:T(128)} %pad_add_fusion.1.pos_ref, bf16[256,512]{1,0:T(8,128)(2,1)} %fusion.20.q_ref, bf16[4,256,512]{2,1,0:T(8,128)(2,1)} %pad_maximum_fusion.2.k_ref.v_ref, bf16[4,256,512]{2,1,0:T(8,128)(2,1)} %pad_maximum_fusion.2.k_ref.v_ref, ...), custom_call_target="tpu_custom_call", output_to_operand_aliasing={{}: (6, {})} | custom-call | flops 1073741824 | bytes 524288 | tf_op jit(solution)/shard_map/pallas_call | solution.py:322
  337.3 7.2 %shard_map.158.rest_0_ = bf16[256,2048]{1,0:T(8,128)(2,1)} custom-call(s32[2]{0:T(128)} %pad_add_fusion.1.pos_ref, bf16[256,512]{1,0:T(8,128)(2,1)} %fusion.23.q_ref, bf16[4,256,512]{2,1,0:T(8,128)(2,1)} %pad_maximum_fusion.2.k_ref.v_ref, bf16[4,256,512]{2,1,0:T(8,128)(2,1)} %pad_maximum_fusion.2.k_ref.v_ref, ...), custom_call_target="tpu_custom_call", output_to_operand_aliasing={{}: (6, {})} | custom-call | flops 1073741824 | bytes 524288 | tf_op jit(solution)/shard_map/pallas_call | solution.py:322
  344.5 7.2 %shard_map.159 = bf16[256,2048]{1,0:T(8,128)(2,1)} custom-call(s32[2]{0:T(128)} %pad_add_fusion.1.pos_ref, bf16[256,512]{1,0:T(8,128)(2,1)} %fusion.27.q_ref, bf16[4,256,512]{2,1,0:T(8,128)(2,1)} %pad_maximum_fusion.2.k_ref.v_ref, bf16[4,256,512]{2,1,0:T(8,128)(2,1)} %pad_maximum_fusion.2.k_ref.v_ref, ...), custom_call_target="tpu_custom_call", output_to_operand_aliasing={{}: (6, {})} | custom-call | flops 1073741824 | bytes 524288 | tf_op jit(solution)/shard_map/pallas_call | solution.py:322
  (128 shorter events, 30.9 us)
Async XLA Ops:
  5.1 19.7 %copy-start.10 = (f32[2048,16]{0,1:T(8,128)S(1)}, f32[2048,16]{0,1:T(8,128)}, u32[]{:S(2)}) copy-start(f32[2048,16]{0,1:T(8,128)} %param.18) | copy-start | bytes 393220
  5.1 24.8 %copy-start.18 = (bf16[256,16]{0,1:T(8,128)(2,1)S(1)}, bf16[256,16]{0,1:T(8,128)(2,1)}, u32[]{:S(2)}) copy-start(bf16[256,16]{0,1:T(8,128)(2,1)} %param.20) | copy-start | bytes 24580
  17.6 5.4 %collective-permute-start = (bf16[16,2304]{1,0:T(8,128)(2,1)S(1)}, bf16[16,2304]{1,0:T(8,128)(2,1)S(1)}, u32[]{:S(2)}, u32[]{:S(2)}) collective-permute-start(bf16[16,2304]{1,0:T(8,128)(2,1)S(1)} %pad_maximum_fusion.4), channel_id=1, source_target_pairs={{0,4},{4,0},{8,12},{12,8},{16,20},{20,16},{24,28},{28,24},{1,5},{5... | collective-permute-start | bytes 221192 | tf_op jit(solution)/shard_map/ppermute | solution.py:366
  25.8 10.6 %collective-permute-start.3 = (bf16[16,2304]{1,0:T(8,128)(2,1)S(1)}, bf16[16,2304]{1,0:T(8,128)(2,1)S(1)}, u32[]{:S(2)}, u32[]{:S(2)}) collective-permute-start(bf16[16,2304]{1,0:T(8,128)(2,1)S(1)} %pad_maximum_fusion.5), channel_id=1, source_target_pairs={{0,8},{4,12},{8,16},{12,20},{16,24},{20,28},{1,9},{5,13},{9,17},{1... | collective-permute-start | bytes 221192 | tf_op jit(solution)/shard_map/ppermute | solution.py:408
  30.6 6.5 %collective-permute-start.2 = (bf16[16,2304]{1,0:T(8,128)(2,1)S(1)}, bf16[16,2304]{1,0:T(8,128)(2,1)S(1)}, u32[]{:S(2)}, u32[]{:S(2)}) collective-permute-start(bf16[16,2304]{1,0:T(8,128)(2,1)S(1)} %pad_maximum_fusion.5), channel_id=1, source_target_pairs={{0,16},{4,20},{8,24},{12,28},{1,17},{5,21},{9,25},{13,29},{2,18},{... | collective-permute-start | bytes 221192 | tf_op jit(solution)/shard_map/ppermute | solution.py:408
  35.1 3.3 collective-permute-start.1
  67.9 12.0 %collective-permute-start.4 = (bf16[256,2048]{1,0:T(8,128)(2,1)}, bf16[256,2048]{1,0:T(8,128)(2,1)S(1)}, u32[]{:S(2)}, u32[]{:S(2)}) collective-permute-start(bf16[256,2048]{1,0:T(8,128)(2,1)} %get-tuple-element.33), channel_id=1, source_target_pairs={{0,1},{1,0},{2,3},{3,2},{4,5},{5,4},{6,7},{7,6},{8,9},{9,8},{10,11... | collective-permute-start | bytes 3145736 | tf_op jit(solution)/shard_map/ppermute | solution.py:372
  79.4 19.4 %collective-permute-start.6 = (bf16[256,2048]{1,0:T(8,128)(2,1)}, bf16[256,2048]{1,0:T(8,128)(2,1)}, u32[]{:S(2)}, u32[]{:S(2)}) collective-permute-start(bf16[256,2048]{1,0:T(8,128)(2,1)} %get-tuple-element.36), channel_id=1, source_target_pairs={{0,1},{1,0},{2,3},{3,2},{4,5},{5,4},{6,7},{7,6},{8,9},{9,8},{10,11... | collective-permute-start | bytes 3145736 | tf_op jit(solution)/shard_map/ppermute | solution.py:372
  79.9 3.5 copy-start.17
  81.9 14.1 %collective-permute-start.5 = (bf16[256,1024]{1,0:T(8,128)(2,1)S(1)}, bf16[256,1024]{1,0:T(8,128)(2,1)S(1)}, u32[]{:S(2)}, u32[]{:S(2)}) collective-permute-start(bf16[256,1024]{1,0:T(8,128)(2,1)S(1)} %slice.265), channel_id=1, source_target_pairs={{0,2},{1,3},{2,0},{3,1},{4,6},{5,7},{6,4},{7,5},{8,10},{9,11},{10,... | collective-permute-start | bytes 1572872 | tf_op jit(solution)/shard_map/ppermute | solution.py:372
  83.7 4.4 %collective-permute-start.8 = (bf16[8192]{0:T(1024)(128)(2,1)S(1)}, bf16[8192]{0:T(1024)(128)(2,1)S(1)}, u32[]{:S(2)}, u32[]{:S(2)}) collective-permute-start(bf16[8192]{0:T(1024)(128)(2,1)S(1)} %dynamic_update_slice.5), channel_id=1, source_target_pairs={{0,1},{1,0},{2,3},{3,2},{4,5},{5,4},{6,7},{7,6},{8,9},{9,8},{10,11... | collective-permute-start | bytes 49160 | tf_op jit(solution)/shard_map/ppermute | solution.py:372
  86.1 51.5 %collective-permute-start.25 = (bf16[1024,512]{1,0:T(8,128)(2,1)}, bf16[1024,512]{1,0:T(8,128)(2,1)}, u32[]{:S(2)}, u32[]{:S(2)}) collective-permute-start(bf16[1024,512]{1,0:T(8,128)(2,1)} %pad_maximum_fusion.1.refs_9_), channel_id=1, source_target_pairs={{0,4},{4,0},{8,12},{12,8},{16,20},{20,16},{24,28},{28,24},{1,5},{5... | collective-permute-start | bytes 3145736 | tf_op jit(solution)/shard_map/ppermute | solution.py:366
  87.6 114.2 %collective-permute-start.20 = (bf16[1024,2048]{1,0:T(8,128)(2,1)}, bf16[1024,2048]{1,0:T(8,128)(2,1)}, u32[]{:S(2)}, u32[]{:S(2)}) collective-permute-start(bf16[1024,2048]{1,0:T(8,128)(2,1)} %refs_9_.7), channel_id=1, source_target_pairs={{0,4},{4,0},{8,12},{12,8},{16,20},{20,16},{24,28},{28,24},{1,5},{5... | collective-permute-start | bytes 12582920 | tf_op jit(solution)/shard_map/ppermute | solution.py:366
  88.1 10.7 %copy-start.8 = (f32[256,2048]{1,0:T(8,128)S(1)}, f32[256,2048]{1,0:T(8,128)}, u32[]{:S(2)}) copy-start(f32[256,2048]{1,0:T(8,128)} %get-tuple-element.35) | copy-start | bytes 6291460
  88.1 13.0 %collective-permute-start.9 = (bf16[8192]{0:T(1024)(128)(2,1)S(1)}, bf16[8192]{0:T(1024)(128)(2,1)S(1)}, u32[]{:S(2)}, u32[]{:S(2)}) collective-permute-start(bf16[8192]{0:T(1024)(128)(2,1)S(1)} %add_dynamic-update-slice_fusion), channel_id=1, source_target_pairs={{0,2},{1,3},{2,0},{3,1},{4,6},{5,7},{6,4},{7,5},{8,10},{9,11},{10,... | collective-permute-start | bytes 49160 | tf_op jit(solution)/shard_map/ppermute | solution.py:372
  97.3 14.9 %collective-permute-start.10 = (bf16[256,1024]{1,0:T(8,128)(2,1)S(1)}, bf16[256,1024]{1,0:T(8,128)(2,1)S(1)}, u32[]{:S(2)}, u32[]{:S(2)}) collective-permute-start(bf16[256,1024]{1,0:T(8,128)(2,1)S(1)} %get-tuple-element.34), channel_id=1, source_target_pairs={{0,2},{1,3},{2,0},{3,1},{4,6},{5,7},{6,4},{7,5},{8,10},{9,11},{10,... | collective-permute-start | bytes 1572872 | tf_op jit(solution)/shard_map/ppermute | solution.py:372
  100.4 21.0 %copy-start.16 = (bf16[256,2048]{1,0:T(8,128)(2,1)S(1)}, bf16[256,2048]{1,0:T(8,128)(2,1)}, u32[]{:S(2)}) copy-start(bf16[256,2048]{1,0:T(8,128)(2,1)} %param.23) | copy-start | bytes 3145732
  100.5 20.9 %collective-permute-start.7 = (bf16[256,1024]{1,0:T(8,128)(2,1)S(1)}, bf16[256,1024]{1,0:T(8,128)(2,1)S(1)}, u32[]{:S(2)}, u32[]{:S(2)}) collective-permute-start(bf16[256,1024]{1,0:T(8,128)(2,1)S(1)} %slice.264), channel_id=1, source_target_pairs={{0,2},{1,3},{2,0},{3,1},{4,6},{5,7},{6,4},{7,5},{8,10},{9,11},{10,... | collective-permute-start | bytes 1572872 | tf_op jit(solution)/shard_map/ppermute | solution.py:372
  121.8 12.2 %collective-permute-start.15 = (bf16[256,1024]{1,0:T(8,128)(2,1)S(1)}, bf16[256,1024]{1,0:T(8,128)(2,1)S(1)}, u32[]{:S(2)}, u32[]{:S(2)}) collective-permute-start(bf16[256,1024]{1,0:T(8,128)(2,1)S(1)} %get-tuple-element.63), channel_id=1, source_target_pairs={{0,2},{1,3},{2,0},{3,1},{4,6},{5,7},{6,4},{7,5},{8,10},{9,11},{10,... | collective-permute-start | bytes 1572872 | tf_op jit(solution)/shard_map/ppermute | solution.py:372
  124.2 16.2 %collective-permute-start.11 = (bf16[256,1024]{1,0:T(8,128)(2,1)}, bf16[256,1024]{1,0:T(8,128)(2,1)S(1)}, u32[]{:S(2)}, u32[]{:S(2)}) collective-permute-start(bf16[256,1024]{1,0:T(8,128)(2,1)} %broadcast_select_fusion.3), channel_id=1, source_target_pairs={{0,0},{1,8},{2,2},{3,10},{4,4},{5,12},{6,6},{7,14},{8,1},{9,9},{10... | collective-permute-start | bytes 1572872 | tf_op jit(solution)/shard_map/ppermute | solution.py:442
  125.9 31.3 %collective-permute-start.12 = (bf16[256,1024]{1,0:T(8,128)(2,1)}, bf16[256,1024]{1,0:T(8,128)(2,1)S(1)}, u32[]{:S(2)}, u32[]{:S(2)}) collective-permute-start(bf16[256,1024]{1,0:T(8,128)(2,1)} %get-tuple-element.64), channel_id=1, source_target_pairs={{0,16},{1,24},{2,18},{3,26},{4,20},{5,28},{6,22},{7,30},{8,17},{9,... | collective-permute-start | bytes 1572872 | tf_op jit(solution)/shard_map/ppermute | solution.py:442
  134.0 1.9 copy-start.9
  135.9 21.3 %collective-permute-start.16 = (bf16[256,1024]{1,0:T(8,128)(2,1)}, bf16[256,1024]{1,0:T(8,128)(2,1)S(1)}, u32[]{:S(2)}, u32[]{:S(2)}) collective-permute-start(bf16[256,1024]{1,0:T(8,128)(2,1)} %get-tuple-element.68), channel_id=1, source_target_pairs={{0,0},{1,8},{2,2},{3,10},{4,4},{5,12},{6,6},{7,14},{8,1},{9,9},{10... | collective-permute-start | bytes 1572872 | tf_op jit(solution)/shard_map/ppermute | solution.py:442
  137.6 36.5 %collective-permute-start.17 = (bf16[256,1024]{1,0:T(8,128)(2,1)}, bf16[256,1024]{1,0:T(8,128)(2,1)S(1)}, u32[]{:S(2)}, u32[]{:S(2)}) collective-permute-start(bf16[256,1024]{1,0:T(8,128)(2,1)} %get-tuple-element.67), channel_id=1, source_target_pairs={{0,16},{1,24},{2,18},{3,26},{4,20},{5,28},{6,22},{7,30},{8,17},{9,... | collective-permute-start | bytes 1572872 | tf_op jit(solution)/shard_map/ppermute | solution.py:442
  140.4 39.4 %copy-start = (bf16[256,1024]{1,0:T(8,128)(2,1)}, bf16[256,1024]{1,0:T(8,128)(2,1)S(1)}, u32[]{:S(2)}) copy-start(bf16[256,1024]{1,0:T(8,128)(2,1)S(1)} %collective-permute-done.11.refs_1_) | copy-start | bytes 1572868
  140.4 37.3 %collective-permute-start.13 = (bf16[256,1024]{1,0:T(8,128)(2,1)S(1)}, bf16[256,1024]{1,0:T(8,128)(2,1)S(1)}, u32[]{:S(2)}, u32[]{:S(2)}) collective-permute-start(bf16[256,1024]{1,0:T(8,128)(2,1)S(1)} %collective-permute-done.11.refs_1_), channel_id=1, source_target_pairs={{0,1},{1,0},{2,3},{3,2},{4,5},{5,4},{6,7},{7,6},{8,9},{9,8},{10,11... | collective-permute-start | bytes 1572872 | tf_op jit(solution)/shard_map/ppermute | solution.py:372
  157.2 22.6 %copy-start.1 = (bf16[256,1024]{1,0:T(8,128)(2,1)}, bf16[256,1024]{1,0:T(8,128)(2,1)S(1)}, u32[]{:S(2)}) copy-start(bf16[256,1024]{1,0:T(8,128)(2,1)S(1)} %collective-permute-done.12.refs_2_) | copy-start | bytes 1572868
  157.2 20.9 %collective-permute-start.14 = (bf16[256,1024]{1,0:T(8,128)(2,1)S(1)}, bf16[256,1024]{1,0:T(8,128)(2,1)S(1)}, u32[]{:S(2)}, u32[]{:S(2)}) collective-permute-start(bf16[256,1024]{1,0:T(8,128)(2,1)S(1)} %collective-permute-done.12.refs_2_), channel_id=1, source_target_pairs={{0,1},{1,0},{2,3},{3,2},{4,5},{5,4},{6,7},{7,6},{8,9},{9,8},{10,11... | collective-permute-start | bytes 1572872 | tf_op jit(solution)/shard_map/ppermute | solution.py:372
  157.2 22.6 %copy-start.2 = (bf16[256,1024]{1,0:T(8,128)(2,1)}, bf16[256,1024]{1,0:T(8,128)(2,1)S(1)}, u32[]{:S(2)}) copy-start(bf16[256,1024]{1,0:T(8,128)(2,1)S(1)} %collective-permute-done.16.refs_5_) | copy-start | bytes 1572868
  157.2 20.9 %collective-permute-start.18 = (bf16[256,1024]{1,0:T(8,128)(2,1)S(1)}, bf16[256,1024]{1,0:T(8,128)(2,1)S(1)}, u32[]{:S(2)}, u32[]{:S(2)}) collective-permute-start(bf16[256,1024]{1,0:T(8,128)(2,1)S(1)} %collective-permute-done.16.refs_5_), channel_id=1, source_target_pairs={{0,1},{1,0},{2,3},{3,2},{4,5},{5,4},{6,7},{7,6},{8,9},{9,8},{10,11... | collective-permute-start | bytes 1572872 | tf_op jit(solution)/shard_map/ppermute | solution.py:372
  174.0 5.7 %copy-start.3 = (bf16[256,1024]{1,0:T(8,128)(2,1)}, bf16[256,1024]{1,0:T(8,128)(2,1)S(1)}, u32[]{:S(2)}) copy-start(bf16[256,1024]{1,0:T(8,128)(2,1)S(1)} %collective-permute-done.17.refs_6_) | copy-start | bytes 1572868
  174.0 4.0 %collective-permute-start.19 = (bf16[256,1024]{1,0:T(8,128)(2,1)S(1)}, bf16[256,1024]{1,0:T(8,128)(2,1)S(1)}, u32[]{:S(2)}, u32[]{:S(2)}) collective-permute-start(bf16[256,1024]{1,0:T(8,128)(2,1)S(1)} %collective-permute-done.17.refs_6_), channel_id=1, source_target_pairs={{0,1},{1,0},{2,3},{3,2},{4,5},{5,4},{6,7},{7,6},{8,9},{9,8},{10,11... | collective-permute-start | bytes 1572872 | tf_op jit(solution)/shard_map/ppermute | solution.py:372
  177.7 2.1 copy-start.4
  177.7 8.9 %collective-permute-start.32 = (f32[256]{0:T(256)S(1)}, f32[256]{0:T(256)S(1)}, u32[]{:S(2)}, u32[]{:S(2)}) collective-permute-start(f32[256]{0:T(256)S(1)} %add_add_fusion), channel_id=1, source_target_pairs={{0,1},{1,0},{2,3},{3,2},{4,5},{5,4},{6,7},{7,6},{8,9},{9,8},{10,11... | collective-permute-start | bytes 3080 | tf_op jit(solution)/shard_map/ppermute | solution.py:372
  178.1 1.7 copy-start.5
  178.1 0.9 copy-start.6
  178.9 0.9 copy-start.7
  186.0 30.2 %collective-permute-start.26 = (bf16[512,512]{1,0:T(8,128)(2,1)}, bf16[512,512]{1,0:T(8,128)(2,1)}, u32[]{:S(2)}, u32[]{:S(2)}) collective-permute-start(bf16[512,512]{1,0:T(8,128)(2,1)} %get-tuple-element.47), channel_id=1, source_target_pairs={{0,8},{4,12},{8,0},{12,4},{16,24},{20,28},{24,16},{28,20},{1,9},{5... | collective-permute-start | bytes 1572872 | tf_op jit(solution)/shard_map/ppermute | solution.py:369
  208.0 9.4 %copy-start.15 = (f32[512,512]{1,0:T(8,128)S(1)}, f32[512,512]{1,0:T(8,128)}, u32[]{:S(2)}) copy-start(f32[512,512]{1,0:T(8,128)} %get-tuple-element.46) | copy-start | bytes 3145732
  208.0 37.8 %collective-permute-start.24 = (bf16[512,512]{1,0:T(8,128)(2,1)}, bf16[512,512]{1,0:T(8,128)(2,1)S(1)}, u32[]{:S(2)}, u32[]{:S(2)}) collective-permute-start(bf16[512,512]{1,0:T(8,128)(2,1)} %get-tuple-element.45), channel_id=1, source_target_pairs={{0,8},{4,12},{8,0},{12,4},{16,24},{20,28},{24,16},{28,20},{1,9},{5... | collective-permute-start | bytes 1572872 | tf_op jit(solution)/shard_map/ppermute | solution.py:369
  214.3 33.4 %collective-permute-start.23 = (bf16[512,512]{1,0:T(8,128)(2,1)}, bf16[512,512]{1,0:T(8,128)(2,1)S(1)}, u32[]{:S(2)}, u32[]{:S(2)}) collective-permute-start(bf16[512,512]{1,0:T(8,128)(2,1)} %get-tuple-element.43), channel_id=1, source_target_pairs={{0,8},{4,12},{8,0},{12,4},{16,24},{20,28},{24,16},{28,20},{1,9},{5... | collective-permute-start | bytes 1572872 | tf_op jit(solution)/shard_map/ppermute | solution.py:369
  217.5 19.9 %collective-permute-start.31 = (bf16[256,512]{1,0:T(8,128)(2,1)S(1)}, bf16[256,512]{1,0:T(8,128)(2,1)}, u32[]{:S(2)}, u32[]{:S(2)}) collective-permute-start(bf16[256,512]{1,0:T(8,128)(2,1)S(1)} %fusion.31), channel_id=1, source_target_pairs={{0,16},{4,20},{8,24},{12,28},{16,0},{20,4},{24,8},{28,12},{1,17},{... | collective-permute-start | bytes 786440 | tf_op jit(solution)/shard_map/ppermute | solution.py:369
  226.5 33.1 %collective-permute-start.22 = (bf16[512,512]{1,0:T(8,128)(2,1)}, bf16[512,512]{1,0:T(8,128)(2,1)}, u32[]{:S(2)}, u32[]{:S(2)}) collective-permute-start(bf16[512,512]{1,0:T(8,128)(2,1)} %get-tuple-element.41), channel_id=1, source_target_pairs={{0,8},{4,12},{8,0},{12,4},{16,24},{20,28},{24,16},{28,20},{1,9},{5... | collective-permute-start | bytes 1572872 | tf_op jit(solution)/shard_map/ppermute | solution.py:369
  234.6 12.9 %copy-start.14 = (f32[512,512]{1,0:T(8,128)S(1)}, f32[512,512]{1,0:T(8,128)}, u32[]{:S(2)}) copy-start(f32[512,512]{1,0:T(8,128)} %get-tuple-element.44) | copy-start | bytes 3145732
  234.6 35.1 %collective-permute-start.21 = (bf16[512,512]{1,0:T(8,128)(2,1)}, bf16[512,512]{1,0:T(8,128)(2,1)S(1)}, u32[]{:S(2)}, u32[]{:S(2)}) collective-permute-start(bf16[512,512]{1,0:T(8,128)(2,1)} %get-tuple-element.39), channel_id=1, source_target_pairs={{0,8},{4,12},{8,0},{12,4},{16,24},{20,28},{24,16},{28,20},{1,9},{5... | collective-permute-start | bytes 1572872 | tf_op jit(solution)/shard_map/ppermute | solution.py:369
  238.5 9.4 %copy-start.12 = (f32[512,512]{1,0:T(8,128)S(1)}, f32[512,512]{1,0:T(8,128)}, u32[]{:S(2)}) copy-start(f32[512,512]{1,0:T(8,128)} %get-tuple-element.42) | copy-start | bytes 3145732
  238.5 35.8 %collective-permute-start.33 = (bf16[256,512]{1,0:T(8,128)(2,1)S(1)}, bf16[256,512]{1,0:T(8,128)(2,1)S(1)}, u32[]{:S(2)}, u32[]{:S(2)}) collective-permute-start(bf16[256,512]{1,0:T(8,128)(2,1)S(1)} %fusion.14), channel_id=1, source_target_pairs={{0,8},{4,12},{8,16},{12,20},{16,24},{20,28},{1,9},{5,13},{9,17},{1... | collective-permute-start | bytes 786440 | tf_op jit(solution)/shard_map/ppermute | solution.py:524
  245.8 70.7 %collective-permute-start.36 = (bf16[256,512]{1,0:T(8,128)(2,1)S(1)}, bf16[256,512]{1,0:T(8,128)(2,1)S(1)}, u32[]{:S(2)}, u32[]{:S(2)}) collective-permute-start(bf16[256,512]{1,0:T(8,128)(2,1)S(1)} %fusion.14), channel_id=1, source_target_pairs={{0,4},{4,0},{8,12},{12,8},{16,20},{20,16},{24,28},{28,24},{1,5},{5... | collective-permute-start | bytes 786440 | tf_op jit(solution)/shard_map/ppermute | solution.py:366
  247.7 15.4 %copy-start.13 = (f32[512,512]{1,0:T(8,128)S(1)}, f32[512,512]{1,0:T(8,128)}, u32[]{:S(2)}) copy-start(f32[512,512]{1,0:T(8,128)} %get-tuple-element.40) | copy-start | bytes 3145732
  247.7 30.5 %collective-permute-start.30 = (bf16[256,512]{1,0:T(8,128)(2,1)S(1)}, bf16[256,512]{1,0:T(8,128)(2,1)S(1)}, u32[]{:S(2)}, u32[]{:S(2)}) collective-permute-start(bf16[256,512]{1,0:T(8,128)(2,1)S(1)} %fusion.30), channel_id=1, source_target_pairs={{0,16},{4,20},{8,24},{12,28},{16,0},{20,4},{24,8},{28,12},{1,17},{... | collective-permute-start | bytes 786440 | tf_op jit(solution)/shard_map/ppermute | solution.py:369
  248.0 26.1 %copy-start.11 = (f32[512,512]{1,0:T(8,128)S(1)}, f32[512,512]{1,0:T(8,128)}, u32[]{:S(2)}) copy-start(f32[512,512]{1,0:T(8,128)} %get-tuple-element.38) | copy-start | bytes 3145732
  259.6 31.4 %collective-permute-start.29 = (bf16[256,512]{1,0:T(8,128)(2,1)S(1)}, bf16[256,512]{1,0:T(8,128)(2,1)S(1)}, u32[]{:S(2)}, u32[]{:S(2)}) collective-permute-start(bf16[256,512]{1,0:T(8,128)(2,1)S(1)} %fusion.29), channel_id=1, source_target_pairs={{0,16},{4,20},{8,24},{12,28},{16,0},{20,4},{24,8},{28,12},{1,17},{... | collective-permute-start | bytes 786440 | tf_op jit(solution)/shard_map/ppermute | solution.py:369
  269.7 26.9 %collective-permute-start.28 = (bf16[256,512]{1,0:T(8,128)(2,1)S(1)}, bf16[256,512]{1,0:T(8,128)(2,1)S(1)}, u32[]{:S(2)}, u32[]{:S(2)}) collective-permute-start(bf16[256,512]{1,0:T(8,128)(2,1)S(1)} %fusion.28), channel_id=1, source_target_pairs={{0,16},{4,20},{8,24},{12,28},{16,0},{20,4},{24,8},{28,12},{1,17},{... | collective-permute-start | bytes 786440 | tf_op jit(solution)/shard_map/ppermute | solution.py:369
  274.2 36.0 %collective-permute-start.27 = (bf16[256,512]{1,0:T(8,128)(2,1)S(1)}, bf16[256,512]{1,0:T(8,128)(2,1)S(1)}, u32[]{:S(2)}, u32[]{:S(2)}) collective-permute-start(bf16[256,512]{1,0:T(8,128)(2,1)S(1)} %fusion.24), channel_id=1, source_target_pairs={{0,16},{4,20},{8,24},{12,28},{16,0},{20,4},{24,8},{28,12},{1,17},{... | collective-permute-start | bytes 786440 | tf_op jit(solution)/shard_map/ppermute | solution.py:369
  278.1 18.5 %collective-permute-start.34 = (bf16[256,512]{1,0:T(8,128)(2,1)S(1)}, bf16[256,512]{1,0:T(8,128)(2,1)S(1)}, u32[]{:S(2)}, u32[]{:S(2)}) collective-permute-start(bf16[256,512]{1,0:T(8,128)(2,1)S(1)} %collective-permute-done.33), channel_id=1, source_target_pairs={{0,8},{4,12},{8,16},{12,20},{16,24},{20,28},{1,9},{5,13},{9,17},{1... | collective-permute-start | bytes 786440 | tf_op jit(solution)/shard_map/ppermute | solution.py:524
  291.0 25.5 %collective-permute-start.37 = (bf16[256,512]{1,0:T(8,128)(2,1)S(1)}, bf16[256,512]{1,0:T(8,128)(2,1)S(1)}, u32[]{:S(2)}, u32[]{:S(2)}) collective-permute-start(bf16[256,512]{1,0:T(8,128)(2,1)S(1)} %collective-permute-done.33), channel_id=1, source_target_pairs={{0,4},{4,0},{8,12},{12,8},{16,20},{20,16},{24,28},{28,24},{1,5},{5... | collective-permute-start | bytes 786440 | tf_op jit(solution)/shard_map/ppermute | solution.py:366
  296.6 16.4 %collective-permute-start.35 = (bf16[256,512]{1,0:T(8,128)(2,1)S(1)}, bf16[256,512]{1,0:T(8,128)(2,1)S(1)}, u32[]{:S(2)}, u32[]{:S(2)}) collective-permute-start(bf16[256,512]{1,0:T(8,128)(2,1)S(1)} %collective-permute-done.34), channel_id=1, source_target_pairs={{0,8},{4,12},{8,16},{12,20},{16,24},{20,28},{1,9},{5,13},{9,17},{1... | collective-permute-start | bytes 786440 | tf_op jit(solution)/shard_map/ppermute | solution.py:524
  310.2 8.9 %collective-permute-start.38 = (bf16[256,512]{1,0:T(8,128)(2,1)S(1)}, bf16[256,512]{1,0:T(8,128)(2,1)S(1)}, u32[]{:S(2)}, u32[]{:S(2)}) collective-permute-start(bf16[256,512]{1,0:T(8,128)(2,1)S(1)} %collective-permute-done.34), channel_id=1, source_target_pairs={{0,4},{4,0},{8,12},{12,8},{16,20},{20,16},{24,28},{28,24},{1,5},{5... | collective-permute-start | bytes 786440 | tf_op jit(solution)/shard_map/ppermute | solution.py:366
  313.0 8.9 %collective-permute-start.39 = (bf16[256,512]{1,0:T(8,128)(2,1)S(1)}, bf16[256,512]{1,0:T(8,128)(2,1)S(1)}, u32[]{:S(2)}, u32[]{:S(2)}) collective-permute-start(bf16[256,512]{1,0:T(8,128)(2,1)S(1)} %collective-permute-done.35), channel_id=1, source_target_pairs={{0,4},{4,0},{8,12},{12,8},{16,20},{20,16},{24,28},{28,24},{1,5},{5... | collective-permute-start | bytes 786440 | tf_op jit(solution)/shard_map/ppermute | solution.py:366
